TPU v7x, 32 devices: a whole 2x2x4 slice. The times are simulated.
32 devices in a mesh: pb: 8 (over z, x), ha: 4 (over y, core).
Axes of the slice: x: 2, y: 2, z: 4, core: 2. Of those that a mesh axis runs over, the one named last changes fastest.
Arguments:
- queries: bfloat16 [1024, 4096], P('pb', 'ha')
- keys: bfloat16 [1024, 4096], P('pb', 'ha')
- values: bfloat16 [1024, 4096], P('pb', 'ha'), may hold values from -6 to 6
- theta: float32 [32, 6, 11], P('ha')
- mix: float32 [32, 4], P('ha')
- gain: float32 [4096], P('ha'), may hold values from 0.5 to 1.5
- out_weight: bfloat16 [4096, 4096], P('ha'), may hold values from -0.09375 to 0.09375
- turn_lengths: int32 [16], replicated, may hold values from 1 to 640, 1024 in all
Outputs:
- output: bfloat16 [1024, 4096], P('pb', 'ha')
Inputs may be any that keep to these rules, and one draw needn't show every extreme that they name: `turn_lengths`: the turns' lengths sum to 1024; the longest turn has exactly 640 positions.
All inputs are finite; a program needn't handle non-finite values.
Results may differ from a plain program's by a relative error of at most 0.018.
Values may be sent and summed in bfloat16 or wider, within the bound.
No kernel may reach another device: no remote copies, remote signals or barrier semaphores. Data moves between devices by JAX's collectives and lax.ppermute only.
A program may use at most 64 MiB of HBM per device.

v0:
```python
import functools
import math

import jax
import jax.numpy as jnp
from jax import lax
from jax.experimental import pallas as pl
from jax.experimental.pallas import tpu as pltpu
from jax.sharding import PartitionSpec as P


GROUP = 4
QCONV = 6
KCONV = 11
MAXBACK = 5
HALO = 16
NEG = -1e30
FLOOR = -5e29


def place():
    me = lax.axis_index("pb")
    side = lax.rem(me, 2)
    return side, me - side


def copy_all(copies, sems):
    started = []
    for n, (src, dst) in enumerate(copies):
        copy = pltpu.make_async_copy(src, dst, sems.at[n])
        copy.start()
        started.append(copy)
    for copy in started:
        copy.wait()


def first_kernel(q_ref, k_ref, v_ref, own_kv, sems):
    side, _ = place()
    rows = q_ref.shape[0]
    half = q_ref.shape[1] // 2
    own = pl.ds(pl.multiple_of(side * half, half), half)
    copy_all(
        [
            (k_ref.at[:, own], own_kv.at[HALO : HALO + rows, :]),
            (v_ref.at[:, own], own_kv.at[HALO + rows : HALO + 2 * rows, :]),
            (q_ref.at[rows - HALO : rows, own], own_kv.at[0:HALO, :]),
        ],
        sems,
    )


def split_kernel(q_ref, k_ref, v_ref, own_q, oth_all, oth_kv, sems):
    side, _ = place()
    rows = q_ref.shape[0]
    half = q_ref.shape[1] // 2
    own = pl.ds(pl.multiple_of(side * half, half), half)
    oth = pl.ds(pl.multiple_of((1 - side) * half, half), half)
    copy_all(
        [
            (k_ref.at[:, oth], oth_kv.at[HALO : HALO + rows, :]),
            (v_ref.at[:, oth], oth_kv.at[HALO + rows : HALO + 2 * rows, :]),
            (q_ref.at[rows - HALO : rows, oth], oth_kv.at[0:HALO, :]),
            (q_ref.at[:, oth], oth_all.at[0:rows, :]),
            (k_ref.at[:, oth], oth_all.at[rows : 2 * rows, :]),
            (v_ref.at[:, oth], oth_all.at[2 * rows : 3 * rows, :]),
            (q_ref.at[:, own], own_q),
        ],
        sems,
    )


def prep_kernel(
    len_ref, theta_ref, mix_ref, gain_ref, out_weight,
    w_ref, start_ref, same_ref, w_own, blend_ref, gain_out, sems, *, scale
):
    reach = (KCONV - 1) // 2
    width = 128
    side_here, first = place()
    copies = load_weights(out_weight, w_own, side_here, sems)
    base = side_here * GROUP
    first_row = first * ((start_ref.shape[0] - HALO) // 2)
    diff = lax.broadcasted_iota(jnp.int32, (width, width), 1) - lax.broadcasted_iota(
        jnp.int32, (width, width), 0
    )

    def body(step, carry):
        h = step // (QCONV // 2)
        q = step % (QCONV // 2)
        for side in range(2):
            lo = jnp.zeros((width, width), jnp.float32)
            hi = jnp.zeros((width, width), jnp.float32)
            tap = 2 * q + side
            for b in range(-reach, reach + 1):
                t = theta_ref[tap, base + h, b + reach] * scale
                lo = jnp.where(diff == b - 64, t, lo)
                hi = jnp.where(diff == b + 64, t, hi)
            w_ref[step, 0:width, side * width : (side + 1) * width] = lo.astype(jnp.bfloat16)
            w_ref[step, width : 2 * width, side * width : (side + 1) * width] = hi.astype(
                jnp.bfloat16
            )
        return carry

    lax.fori_loop(0, GROUP * QCONV // 2, body, 0)
    for p in range(GROUP):
        for h in range(GROUP):
            n = p * GROUP + h
            blend_ref[n : n + 1, :] = jnp.full((1, width), mix_ref[p, base + h], jnp.float32)
    half = gain_out.shape[1]
    gain_out[...] = gain_ref[:, pl.ds(pl.multiple_of(side_here * half, half), half)]
    shape = start_ref.shape
    row = first_row - HALO + lax.broadcasted_iota(jnp.int32, shape, 0)
    start = jnp.zeros(shape, jnp.int32)
    begin = jnp.int32(0)
    for n in range(len_ref.shape[0]):
        start = jnp.where(row >= begin, begin, start)
        begin = begin + len_ref[n]
    start_ref[...] = start
    for a in range(1, QCONV):
        same_ref[a - 1] = (row[HALO:] - a >= start[HALO:]).astype(jnp.float32)
    for copy in copies:
        copy.wait()


def window_masks(col0, first_row, row0, n_rows, start, score_ok, bias):
    n_ext = n_rows + HALO
    lane = lax.broadcasted_iota(jnp.int32, (1, 128), 1)
    start_ext = start[pl.ds(row0, n_ext), :]
    row_ext = first_row + row0 - HALO + lax.broadcasted_iota(jnp.int32, (n_ext, 128), 0)
    for t in range(3):
        col = col0 + t * 128 + lane
        ok = (col >= start_ext) & (col <= row_ext)
        score_ok[t] = jnp.where(ok, 1.0, 0.0)
    for t in range(2):
        col = col0 + 64 + t * 128 + lane
        ok = (col >= start_ext[HALO:]) & (col <= row_ext[HALO:])
        bias[t] = jnp.where(ok, 0.0, NEG)


def reaches(start, row0, col0):
    return jnp.min(start[row0 + HALO : row0 + HALO + 8, :]) < col0 + 64 + 256


def one_window(at, row0, n_rows, qs, ks, vs, w, same, work, state, result):
    score_ok, bias, lhs, ps, probs, factors = work
    peak, total, acc = state
    peak_out, total_out, acc_out = result
    n_ext = n_rows + HALO
    dh = 128
    n_q = QCONV // 2
    step = 64

    def scores(h):
        cols = slice(h * dh, (h + 1) * dh)
        buf = h % 2
        s = lax.dot_general(
            qs[pl.ds(row0, n_ext), cols],
            ks[pl.ds(at, 384), cols],
            (((1,), (1,)), ((), ())),
            preferred_element_type=jnp.float32,
        )
        for t in range(3):
            piece = (s[:, t * 128 : (t + 1) * 128] * score_ok[t]).astype(jnp.bfloat16)
            if t < 2:
                lhs[buf, 0:n_ext, t * 128 : (t + 1) * 128] = piece
            if t > 0:
                lhs[buf, n_ext : 2 * n_ext, (t - 1) * 128 : t * 128] = piece

    def taps(h, q):
        buf = h % 2
        pair = jnp.dot(lhs[buf], w[h * n_q + q], preferred_element_type=jnp.float32)
        ps[buf, 2 * q] = pair[:, 0:128]
        ps[buf, 2 * q + 1] = pair[:, 128:256]

    def weigh(h, r):
        buf = h % 2
        rows = pl.ds(row0 + r, step)
        keep = [same[a - 1, rows, :] for a in range(1, QCONV)]
        parts = []
        for t in range(2):
            base = t * n_ext + HALO + r
            conv = ps[buf, 0, base : base + step, :] + bias[t, r : r + step, :]
            for a in range(1, QCONV):
                conv = conv + ps[buf, a, base - a : base - a + step, :] * keep[a - 1]
            parts.append(conv)
        old = peak[h, rows, :]
        top = jnp.max(jnp.maximum(parts[0], parts[1]), axis=1, keepdims=True)
        new = jnp.maximum(old, top)
        ws = [jnp.exp(c - new) for c in parts]
        factor = jnp.exp(old - new)
        if peak_out is not None:
            peak_out[h, rows, :] = new
        out_rows = rows if peak_out is not None else pl.ds(r, step)
        total_out[h, out_rows, :] = total[h, rows, :] * factor + jnp.sum(
            ws[0] + ws[1], axis=1, keepdims=True
        )
        factors[buf, r : r + step, :] = factor
        for t in range(2):
            probs[buf, r : r + step, t * 128 : (t + 1) * 128] = ws[t].astype(jnp.bfloat16)

    def gather(h):
        buf = h % 2
        out_rows = pl.ds(row0, n_rows) if peak_out is not None else pl.ds(0, n_rows)
        upd = jnp.dot(
            probs[buf], vs[pl.ds(at + 64, 256), :], preferred_element_type=jnp.float32
        )
        factor = factors[buf]
        for t in range(GROUP):
            c = slice(t * dh, (t + 1) * dh)
            acc_out[h, out_rows, c] = acc[h, pl.ds(row0, n_rows), c] * factor + upd[:, c]

    chunks = list(range(0, n_rows, step))
    scores(0)
    for q in range(n_q):
        taps(0, q)
    for h in range(GROUP):
        more = h + 1 < GROUP
        if more:
            scores(h + 1)
        for n in range(max(len(chunks), n_q)):
            if n < len(chunks):
                weigh(h, chunks[n])
            if more and n < n_q:
                taps(h + 1, n)
        gather(h)


def put(src, lo, ks, vs, blk):
    rows = (src.shape[0] - lo) // 2
    at = pl.ds(pl.multiple_of(blk * rows, rows), rows)
    ks[at, :] = src[lo : lo + rows, :]
    vs[at, :] = src[lo + rows : lo + 2 * rows, :]


def load_weights(out_weight, dst, who, sems):
    half, part = dst.shape[1:]
    ha = lax.axis_index("ha")
    core = lax.rem(ha, 2)
    pair = ha - core
    away = 2 - pair
    order = (away + 1 - core, away + core, pair + 1 - core, ha)
    copies = []
    for n in range(dst.shape[0]):
        rows = pl.ds(pl.multiple_of(who * half, half), half)
        cols = pl.ds(pl.multiple_of(order[n] * part, part), part)
        copy = pltpu.make_async_copy(out_weight.at[rows, cols], dst.at[n], sems.at[n])
        copy.start()
        copies.append(copy)
    return copies


def own_kernel(
    own_q, own_kv, swap, out_weight, w, start, same,
    qs, ks, vs, peak, total, acc, w_oth, e_src, score_ok, bias, lhs, ps, probs, factors, sems
):
    rows, half = own_q.shape
    side, first = place()
    first_row = first * rows
    copies = load_weights(out_weight, w_oth, 1 - side, sems)
    qs[pl.ds(pl.multiple_of(HALO + side * rows, HALO), rows), :] = own_q[...]
    qs[pl.ds(pl.multiple_of(HALO + (1 - side) * rows, HALO), rows), :] = swap[0:rows, :]

    qs[0:HALO, :] = jnp.zeros((HALO, half), jnp.bfloat16)

    @pl.when(side == 0)
    def _():
        e_src[...] = swap[rows : 3 * rows, :]

    @pl.when(side == 1)
    def _():
        e_src[...] = own_kv[HALO : HALO + 2 * rows, :]

    zero = jnp.zeros((rows, half), jnp.bfloat16)
    for blk in (0, 1, 8):
        ks[blk * rows : (blk + 1) * rows, :] = zero
        vs[blk * rows : (blk + 1) * rows, :] = zero
    put(own_kv, HALO, ks, vs, 6 + side)
    put(swap, rows, ks, vs, 7 - side)
    peak[...] = jnp.full(peak.shape, FLOOR, jnp.float32)
    total[...] = jnp.zeros(total.shape, jnp.float32)
    acc[...] = jnp.zeros(acc.shape, jnp.float32)
    state = (peak, total, acc)
    window_masks(first_row, first_row, 0, 2 * rows, start, score_ok, bias)
    one_window(
        6 * rows, 0, 2 * rows, qs, ks, vs, w, same,
        (score_ok, bias, lhs, ps, probs, factors), state, state,
    )
    for copy in copies:
        copy.wait()


def next_kernel(
    pa, pb, w, start, same, qs_in, ks_in, vs_in, peak_in, total_in, acc_in,
    qs, ks, vs, peak, total, acc, score_ok, bias, lhs, ps, probs, factors
):
    rows = (qs.shape[0] - HALO) // 2
    side, first = place()
    first_row = first * rows
    put(pa, HALO, ks, vs, 4 + side)
    put(pb, HALO, ks, vs, 5 - side)

    @pl.when(side == 0)
    def _():
        qs[0:HALO, :] = pb[0:HALO, :]

    @pl.when(side == 1)
    def _():
        qs[0:HALO, :] = pa[0:HALO, :]

    state = (peak, total, acc)
    window_masks(first_row - 2 * rows, first_row, 0, 2 * rows, start, score_ok, bias)
    one_window(
        4 * rows, 0, 2 * rows, qs, ks, vs, w, same,
        (score_ok, bias, lhs, ps, probs, factors), state, state,
    )


def mid_kernel(
    fa, fb, w, start, same, qs, ks_in, vs_in, peak_in, total_in, acc_in,
    ks, vs, peak, total, acc, score_ok, bias, lhs, ps, probs, factors
):
    rows = (qs.shape[0] - HALO) // 2
    side, first = place()
    first_row = first * rows
    put(fa, HALO, ks, vs, 2 + side)
    put(fb, HALO, ks, vs, 3 - side)
    state = (peak, total, acc)

    @pl.when(reaches(start, 0, first_row - 4 * rows))
    def _():
        window_masks(first_row - 4 * rows, first_row, 0, 2 * rows, start, score_ok, bias)
        one_window(
            2 * rows, 0, 2 * rows, qs, ks, vs, w, same,
            (score_ok, bias, lhs, ps, probs, factors), state, state,
        )


def finish_rows(
    mix_ref, gain_ref, row0, out_ref, ks, vs, w, start, same, qs, peak, total, acc,
    score_ok, bias, lhs, ps, probs, factors, total_end, acc_end
):
    rows, half = out_ref.shape
    _, first = place()
    first_row = first * rows
    dh = half // GROUP
    needed = reaches(start, row0, first_row - 6 * rows)

    @pl.when(needed)
    def _():
        window_masks(first_row - 6 * rows, first_row, row0, rows, start, score_ok, bias)
        one_window(
            0, row0, rows, qs, ks, vs, w, same, (score_ok, bias, lhs, ps, probs, factors),
            (peak, total, acc), (None, total_end, acc_end),
        )

    @pl.when(jnp.logical_not(needed))
    def _():
        total_end[...] = total[:, row0 : row0 + rows, :]
        acc_end[...] = acc[:, row0 : row0 + rows, :]

    inverse = [1.0 / total_end[p] for p in range(GROUP)]
    for h in range(GROUP):
        cols = slice(h * dh, (h + 1) * dh)
        out = jnp.zeros((rows, dh), jnp.float32)
        for p in range(GROUP):
            n = p * GROUP + h
            out = out + mix_ref[n : n + 1, :] * (acc_end[p, :, cols] * inverse[p])
        mean_sq = jnp.mean(out * out, axis=1, keepdims=True)
        out_ref[:, cols] = (out * lax.rsqrt(mean_sq + 1e-06) * gain_ref[:, cols]).astype(
            jnp.bfloat16
        )


def odd_kernel(
    mix_ref, gain_ref, w, start, same, qs, ks, vs, peak, total, acc,
    out_ref, score_ok, bias, lhs, ps, probs, factors, total_end, acc_end
):
    finish_rows(
        mix_ref, gain_ref, out_ref.shape[0], out_ref, ks, vs, w, start, same, qs, peak, total,
        acc, score_ok, bias, lhs, ps, probs, factors, total_end, acc_end,
    )


def even_kernel(
    mix_ref, gain_ref, odd_ref, last, w, start, same, qs, ks_in, vs_in, peak, total, acc,
    mine_ref, theirs_ref, ks, vs,
    score_ok, bias, lhs, ps, probs, factors, total_end, acc_end, even_ref
):
    side, _ = place()
    put(last, 0, ks, vs, 1)
    finish_rows(
        mix_ref, gain_ref, 0, even_ref, ks, vs, w, start, same, qs, peak, total,
        acc, score_ok, bias, lhs, ps, probs, factors, total_end, acc_end,
    )

    @pl.when(side == 0)
    def _():
        mine_ref[...] = even_ref[...]
        theirs_ref[...] = odd_ref[...]

    @pl.when(side == 1)
    def _():
        mine_ref[...] = odd_ref[...]
        theirs_ref[...] = even_ref[...]


def own_part_kernel(x_ref, w_ref, out_ref):
    for n in range(w_ref.shape[0]):
        out_ref[n] = jnp.dot(x_ref[...], w_ref[n], preferred_element_type=jnp.float32)


def add_part_kernel(x_ref, w_ref, part_ref, give_ref, keep_ref, *, lo):
    for n, out_ref in enumerate((give_ref, keep_ref)):
        out = jnp.dot(x_ref[...], w_ref[lo + n], preferred_element_type=jnp.float32)
        out_ref[...] = (out + part_ref[lo + n]).astype(jnp.bfloat16)


def from_behind(block, axis, distance):
    devices = range(lax.axis_size(axis))
    route = [(i - distance, i) for i in devices if i - distance in devices]
    return lax.ppermute(block, axis, route)


def conv_block(scores, theta_part, row_pos, row_start, col_pos, out_cols):
    rim_rows = QCONV - 1
    count_rows = row_pos.shape[0]
    conv_sum = jnp.zeros((scores.shape[0], count_rows, out_cols), jnp.float32)
    above_start = col_pos[None, :] >= row_start[:, None]
    for offset_q in range(QCONV):
        allowed = above_start & (col_pos[None, :] <= row_pos[:, None] - offset_q)
        taken_rows = jnp.where(
            allowed[None],
            scores[:, rim_rows - offset_q : rim_rows - offset_q + count_rows, :],
            jnp.float32(0.0),
        )
        for offset_k in range(KCONV):
            conv_sum = (
                conv_sum
                + theta_part[:, offset_q, KCONV - 1 - offset_k][:, None, None]
                * taken_rows[:, :, offset_k : offset_k + out_cols]
            )
    return conv_sum


def general_plan(queries, keys, values, theta, mix, gain, out_weight, turn_lengths):
    tile_rows = queries.shape[0]
    feature_cols = queries.shape[1]
    local_heads = theta.shape[0]
    head_size = feature_cols // local_heads
    groups = local_heads // GROUP
    group_cols = GROUP * head_size
    rim_rows = QCONV - 1
    key_reach = (KCONV - 1) // 2
    tile_index = lax.axis_index("pb")
    first_row = tile_index * tile_rows
    starts = jnp.cumsum(turn_lengths) - turn_lengths
    row_pos = first_row + jnp.arange(tile_rows, dtype=jnp.int32)
    row_start = jnp.max(jnp.where(starts[None, :] <= row_pos[:, None], starts[None, :], 0), axis=1)
    earlier = from_behind(queries[tile_rows - rim_rows :], "pb", 1)
    query_ext = jnp.concatenate([earlier, queries], 0).reshape(
        tile_rows + rim_rows, local_heads, head_size
    )
    kv_pair = jnp.stack([keys, values], 0)
    window = kv_pair[None]
    while window.shape[0] < MAXBACK + 1:
        have_count = window.shape[0]
        take_count = min(have_count, MAXBACK + 1 - have_count)
        moved_runs = from_behind(window[have_count - take_count :], "pb", have_count)
        window = jnp.concatenate([moved_runs, window], 0)
    key_span = (MAXBACK + 1) * tile_rows
    key_win = window[:, 0].reshape(key_span, feature_cols)
    val_win = window[:, 1].reshape(key_span, feature_cols)
    key_pad = jnp.pad(key_win, ((key_reach, key_reach), (0, 0))).reshape(
        key_span + 2 * key_reach, local_heads, head_size
    )
    key_base = first_row - MAXBACK * tile_rows
    score_scale = 1.0 / math.sqrt(head_size)
    state_carry = (
        jnp.full((local_heads, tile_rows), -1e30, jnp.float32),
        jnp.zeros((local_heads, tile_rows), jnp.float32),
        jnp.zeros((local_heads, tile_rows, group_cols), jnp.float32),
    )
    for block_num in range(MAXBACK + 1):
        block_row_peak, block_row_total, block_accumulated = state_carry
        lower = block_num * tile_rows
        key_slice = key_pad[lower : lower + tile_rows + 2 * key_reach]
        scores = (
            jnp.einsum("rhd,chd->hrc", query_ext, key_slice, preferred_element_type=jnp.float32)
            * score_scale
        )
        col_pos = (
            key_base + lower - key_reach + jnp.arange(tile_rows + 2 * key_reach, dtype=jnp.int32)
        )
        conv_sum = conv_block(scores, theta, row_pos, row_start, col_pos, tile_rows)
        key_pos = key_base + lower + jnp.arange(tile_rows, dtype=jnp.int32)
        keep_mask = (key_pos[None, :] >= row_start[:, None]) & (
            key_pos[None, :] <= row_pos[:, None]
        )
        masked = jnp.where(keep_mask[None], conv_sum, jnp.float32(-1e30))
        new_peak = jnp.maximum(block_row_peak, jnp.max(masked, axis=-1))
        weights = jnp.where(
            keep_mask[None], jnp.exp(conv_sum - new_peak[..., None]), jnp.float32(0.0)
        )
        factor = jnp.exp(block_row_peak - new_peak)
        new_total = block_row_total * factor + jnp.sum(weights, axis=-1)
        prob_bf = weights.astype(jnp.bfloat16).reshape(groups, GROUP, tile_rows, tile_rows)
        val_block = val_win[lower : lower + tile_rows].reshape(tile_rows, groups, group_cols)
        update = jnp.einsum(
            "gpij,jgc->gpic", prob_bf, val_block, preferred_element_type=jnp.float32
        )
        update = update.reshape(local_heads, tile_rows, group_cols)
        state_carry = (new_peak, new_total, block_accumulated * factor[..., None] + update)
    _, row_total, accumulated = state_carry
    normalized = (accumulated / row_total[..., None]).reshape(
        groups, GROUP, tile_rows, GROUP, head_size
    )
    mix_grid = mix.reshape(groups, GROUP, GROUP)
    head_out = jnp.einsum("gkp,gpikd->gikd", mix_grid, normalized)
    head_out = jnp.transpose(head_out, (1, 0, 2, 3)).reshape(tile_rows, local_heads, head_size)
    mean_sq = jnp.mean(head_out * head_out, axis=-1, keepdims=True)
    normed = (
        (head_out * lax.rsqrt(mean_sq + 1e-06) * gain.reshape(local_heads, head_size))
        .reshape(tile_rows, feature_cols)
        .astype(jnp.bfloat16)
    )
    summed = lax.psum_scatter(
        lax.dot_general(
            out_weight, normed, (((0,), (1,)), ((), ())), preferred_element_type=jnp.float32
        ).astype(jnp.bfloat16),
        "ha",
        scatter_dimension=0,
        tiled=True,
    ).astype(jnp.float32)
    return summed.T.astype(jnp.bfloat16)


def paired_plan(queries, keys, values, theta, mix, gain, out_weight, turn_lengths):
    rows, feats = queries.shape
    half = feats // 2
    heads = theta.shape[0]
    dh = feats // heads
    n_pb = lax.axis_size("pb")
    n_ha = lax.axis_size("ha")
    vm = pl.BlockSpec(memory_space=pltpu.VMEM)
    sm = pl.BlockSpec(memory_space=pltpu.SMEM)
    hbm = pl.BlockSpec(memory_space=pltpu.HBM)
    stay = functools.partial(pltpu.with_memory_space_constraint, memory_space=pltpu.HBM)
    small = pltpu.CompilerParams(vmem_limit_bytes=8 * 1024 * 1024)
    bf = jnp.bfloat16
    f32 = jnp.float32
    kv_rows = 2 * rows + HALO
    n_rows = 2 * rows
    n_ext = n_rows + HALO
    on_chip = pltpu.VMEM
    params = pltpu.CompilerParams(vmem_limit_bytes=24 * 1024 * 1024)

    inputs = (stay(queries), stay(keys), stay(values))
    own_kv = pl.pallas_call(
        first_kernel,
        out_shape=on_chip((kv_rows, half), bf),
        in_specs=[hbm] * 3,
        out_specs=vm,
        scratch_shapes=[pltpu.SemaphoreType.DMA((3,))],
        compiler_params=small,
    )(*inputs)
    own_q, oth_all, oth_kv = pl.pallas_call(
        split_kernel,
        out_shape=(
            on_chip((rows, half), bf),
            on_chip((3 * rows, half), bf),
            on_chip((kv_rows, half), bf),
        ),
        in_specs=[hbm] * 3,
        out_specs=(vm, vm, vm),
        scratch_shapes=[pltpu.SemaphoreType.DMA((7,))],
        compiler_params=small,
    )(*inputs)

    pairs = range(n_pb)
    up = [(i, i + 2) for i in pairs if i + 2 < n_pb]
    cross = [(i, (i ^ 1) + 2) for i in pairs if (i ^ 1) + 2 < n_pb]
    swap_route = [(i, i ^ 1) for i in pairs]
    far = [(i, i + MAXBACK + 1) for i in pairs if i + MAXBACK + 1 < n_pb]

    pa = lax.ppermute(own_kv, "pb", up)
    pbk = lax.ppermute(oth_kv, "pb", cross)
    swap = lax.ppermute(oth_all, "pb", swap_route)

    n_pair = GROUP * QCONV // 2
    cols = out_weight.shape[1]
    part = cols // n_ha
    weights = on_chip((n_ha, half, part), bf)
    heavy = stay(out_weight)
    prep_params = pltpu.CompilerParams(vmem_limit_bytes=16 * 1024 * 1024)
    w, start, same, w_own, blend, gain_own = pl.pallas_call(
        functools.partial(prep_kernel, scale=1.0 / math.sqrt(dh)),
        out_shape=(
            on_chip((n_pair, 256, 256), bf),
            on_chip((n_ext, 128), jnp.int32),
            on_chip((QCONV - 1, n_rows, 128), f32),
            weights,
            on_chip((GROUP * GROUP, 128), f32),
            on_chip((1, half), f32),
        ),
        in_specs=[sm, sm, sm, vm, hbm],
        out_specs=(vm,) * 6,
        scratch_shapes=[pltpu.SemaphoreType.DMA((n_ha,))],
        compiler_params=prep_params,
        cost_estimate=pl.CostEstimate(
            flops=20_000_000, bytes_accessed=2_400_000, transcendentals=0
        ),
    )(stay(turn_lengths), stay(theta.transpose(1, 0, 2)), stay(mix.T), stay(gain.reshape(1, -1)), heavy)
    pa, w = lax.optimization_barrier((pa, w))
    fa = lax.ppermute(pa, "pb", up)
    fb = lax.ppermute(pbk, "pb", up)

    def state(make):
        return (
            make((GROUP, n_rows, 128), f32),
            make((GROUP, n_rows, 128), f32),
            make((GROUP, n_rows, half), f32),
        )

    def work(count):
        ext = count + HALO
        return [
            pltpu.VMEM((3, ext, 128), f32),
            pltpu.VMEM((2, count, 128), f32),
            pltpu.VMEM((2, 2 * ext, 256), bf),
            pltpu.VMEM((2, QCONV, 2 * ext, 128), f32),
            pltpu.VMEM((2, count, 256), bf),
            pltpu.VMEM((2, count, 128), f32),
        ]

    def cost(n):
        return pl.CostEstimate(
            flops=int(n * 1_500_000_000),
            bytes_accessed=int(n * 6_000_000),
            transcendentals=int(n * 300_000),
        )

    span = on_chip((9 * rows, half), bf)
    qs, ks, vs, peak, total, acc, w_oth, e_src = pl.pallas_call(
        own_kernel,
        out_shape=(on_chip((n_ext, half), bf), span, span)
        + state(on_chip)
        + (weights, on_chip((2 * rows, half), bf)),
        in_specs=[vm] * 3 + [hbm] + [vm] * 3,
        out_specs=(vm,) * 8,
        scratch_shapes=work(n_rows) + [pltpu.SemaphoreType.DMA((n_ha,))],
        compiler_params=params,
        cost_estimate=cost(1),
    )(own_q, own_kv, swap, heavy, w, start, same)
    last = lax.ppermute(e_src, "pb", far)
    qs, ks, vs, peak, total, acc = pl.pallas_call(
        next_kernel,
        out_shape=(on_chip((n_ext, half), bf), span, span) + state(on_chip),
        in_specs=[vm] * 11,
        out_specs=(vm,) * 6,
        input_output_aliases={5: 0, 6: 1, 7: 2, 8: 3, 9: 4, 10: 5},
        scratch_shapes=work(n_rows),
        compiler_params=params,
        cost_estimate=cost(1),
    )(pa, pbk, w, start, same, qs, ks, vs, peak, total, acc)
    ks, vs, peak, total, acc = pl.pallas_call(
        mid_kernel,
        out_shape=(span, span) + state(on_chip),
        in_specs=[vm] * 11,
        out_specs=(vm,) * 5,
        input_output_aliases={6: 0, 7: 1, 8: 2, 9: 3, 10: 4},
        scratch_shapes=work(n_rows),
        compiler_params=params,
        cost_estimate=cost(1),
    )(fa, fb, w, start, same, qs, ks, vs, peak, total, acc)
    ends = [pltpu.VMEM((GROUP, rows, 128), f32), pltpu.VMEM((GROUP, rows, half), f32)]
    odd = pl.pallas_call(
        odd_kernel,
        out_shape=on_chip((rows, half), bf),
        in_specs=[vm] * 11,
        out_specs=vm,
        scratch_shapes=work(rows) + ends,
        compiler_params=params,
        cost_estimate=cost(0.5),
    )(blend, gain_own, w, start, same, qs, ks, vs, peak, total, acc)
    last, odd = lax.optimization_barrier((last, odd))
    mine, theirs, _, _ = pl.pallas_call(
        even_kernel,
        out_shape=(on_chip((rows, half), bf),) * 2 + (span, span),
        in_specs=[vm] * 13,
        out_specs=(vm,) * 4,
        input_output_aliases={8: 2, 9: 3},
        scratch_shapes=work(rows) + ends + [pltpu.VMEM((rows, half), bf)],
        compiler_params=params,
        cost_estimate=cost(0.5),
    )(blend, gain_own, odd, last, w, start, same, qs, ks, vs, peak, total, acc)
    got = lax.ppermute(theirs, "pb", swap_route)

    own_part = pl.pallas_call(
        own_part_kernel,
        out_shape=on_chip((n_ha, rows, part), f32),
        in_specs=[vm, vm],
        out_specs=vm,
        compiler_params=params,
        cost_estimate=pl.CostEstimate(
            flops=2 * rows * half * cols, bytes_accessed=8_000_000, transcendentals=0
        ),
    )(mine, w_own)

    def finish(lo, got):
        return pl.pallas_call(
            functools.partial(add_part_kernel, lo=lo),
            out_shape=(on_chip((rows, part), bf), on_chip((rows, part), bf)),
            in_specs=[vm, vm, vm],
            out_specs=(vm, vm),
            compiler_params=params,
            cost_estimate=pl.CostEstimate(
                flops=rows * half * cols, bytes_accessed=4_000_000, transcendentals=0
            ),
        )(got, w_oth, own_part)

    near_route = [(i, i ^ 1) for i in range(n_ha)]
    give, keep = finish(0, got)
    take = lax.ppermute(give, "ha", near_route)
    away = (keep.astype(f32) + take.astype(f32)).astype(bf)
    arrived = lax.ppermute(away, "ha", [(i, i ^ 2) for i in range(n_ha)])
    give, keep = finish(2, got)
    take = lax.ppermute(give, "ha", near_route)
    here = keep.astype(f32) + take.astype(f32)
    return (here + arrived.astype(f32)).astype(bf)


def per_device(queries, keys, values, theta, mix, gain, out_weight, turn_lengths):
    rows, feats = queries.shape
    heads = theta.shape[0]
    fits = rows == 128 and feats == 128 * heads and heads == 2 * GROUP
    n_pb, n_ha = lax.axis_size("pb"), lax.axis_size("ha")
    fits = fits and n_pb % 2 == 0 and n_ha == 4
    args = (queries, keys, values, theta, mix, gain, out_weight, turn_lengths)
    if not fits:
        return general_plan(*args)
    return paired_plan(*args)


def solution(mesh):
    return jax.shard_map(
        per_device,
        mesh=mesh,
        in_specs=(
            P("pb", "ha"),
            P("pb", "ha"),
            P("pb", "ha"),
            P("ha", None, None),
            P("ha", None),
            P("ha"),
            P("ha", None),
            P(),
        ),
        out_specs=P("pb", "ha"),
        check_vma=False,
    )
```

profile of v0, /device:TPU:28, one launch (start us, length us, event | category | flops | bytes accessed | tf_op | source)
XLA Modules:
  0.0 59.6 jit_solution(15317223876375080552)
XLA Ops:
  0.0 1.3 %shard_map.83 = (bf16[128,512]{1,0:T(8,128)(2,1)S(1)}, bf16[384,512]{1,0:T(8,128)(2,1)S(1)}, bf16[272,512]{1,0:T(8,128)(2,1)S(1)}) custom-call(bf16[128,1024]{1,0:T(8,128)(2,1)} %q_ref.3, bf16[128,1024]{1,0:T(8,128)(2,1)} %k_ref.3, bf16[128,1024]{1,0:T(8,128)(2,1)} %v_ref.3), custom_call_target="tpu_custom_call" | custom-call | tf_op jit(solution)/shard_map/pallas_call | solution.py:565
  1.3 1.6 %collective-permute-start = (bf16[384,512]{1,0:T(8,128)(2,1)S(1)}, bf16[384,512]{1,0:T(8,128)(2,1)S(1)}, u32[]{:S(2)}, u32[]{:S(2)}) collective-permute-start(bf16[384,512]{1,0:T(8,128)(2,1)S(1)} %get-tuple-element.46), channel_id=1, source_target_pairs={{0,4},{4,0},{8,12},{12,8},{16,20},{20,16},{24,28},{28,24},{1,5},{5... | collective-permute-start | bytes 1179656 | tf_op jit(solution)/shard_map/ppermute | solution.py:586
  2.8 1.0 %shard_map.84.own_kv = bf16[272,512]{1,0:T(8,128)(2,1)S(1)} custom-call(bf16[128,1024]{1,0:T(8,128)(2,1)} %q_ref.3, bf16[128,1024]{1,0:T(8,128)(2,1)} %k_ref.3, bf16[128,1024]{1,0:T(8,128)(2,1)} %v_ref.3), custom_call_target="tpu_custom_call" | custom-call | tf_op jit(solution)/shard_map/pallas_call | solution.py:557
  3.8 1.3 %collective-permute-start.1 = (bf16[272,512]{1,0:T(8,128)(2,1)S(1)}, bf16[272,512]{1,0:T(8,128)(2,1)S(1)}, u32[]{:S(2)}, u32[]{:S(2)}) collective-permute-start(bf16[272,512]{1,0:T(8,128)(2,1)S(1)} %shard_map.84.own_kv), channel_id=1, source_target_pairs={{0,8},{4,12},{8,16},{12,20},{16,24},{20,28},{1,9},{5,13},{9,17},{1... | collective-permute-start | bytes 835592 | tf_op jit(solution)/shard_map/ppermute | solution.py:584
  5.1 1.3 %collective-permute-start.3 = (bf16[272,512]{1,0:T(8,128)(2,1)S(1)}, bf16[272,512]{1,0:T(8,128)(2,1)S(1)}, u32[]{:S(2)}, u32[]{:S(2)}) collective-permute-start(bf16[272,512]{1,0:T(8,128)(2,1)S(1)} %get-tuple-element.53), channel_id=1, source_target_pairs={{0,12},{4,8},{8,20},{12,16},{16,28},{20,24},{1,13},{5,9},{9,21},{1... | collective-permute-start | bytes 835592 | tf_op jit(solution)/shard_map/ppermute | solution.py:585
  6.4 3.3 %shard_map.82 = (bf16[12,256,256]{2,1,0:T(8,128)(2,1)S(1)}, s32[272,128]{1,0:T(8,128)S(1)}, f32[5,256,128]{2,1,0:T(8,128)S(1)}, bf16[4,512,1024]{2,1,0:T(8,128)(...) custom-call(s32[16]{0:T(128)} %len_ref.1, f32[6,8,11]{2,1,0:T(8,128)} %bitcast.3, f32[4,8]{1,0:T(4,128)} %bitcast.5, ...), custom_call_target="tpu_custom_call" | custom-call | flops 20000000 | bytes 2400000 | tf_op jit(solution)/shard_map/pallas_call | solution.py:594
  9.8 5.5 %collective-permute-done.1.pa = bf16[272,512]{1,0:T(8,128)(2,1)S(1)} collective-permute-done((bf16[272,512]{1,0:T(8,128)(2,1)S(1)}, bf16[272,512]{1,0:T(8,128)(2,1)S(1)}, u32[]{:S(2)}, u32[]{:S(2)}) %collective-permute-start.1) | collective-permute-done | bytes 278560 | tf_op jit(solution)/shard_map/ppermute | solution.py:584
  15.3 1.3 %collective-permute-start.4 = (bf16[272,512]{1,0:T(8,128)(2,1)S(1)}, bf16[272,512]{1,0:T(8,128)(2,1)S(1)}, u32[]{:S(2)}, u32[]{:S(2)}) collective-permute-start(bf16[272,512]{1,0:T(8,128)(2,1)S(1)} %collective-permute-done.1.pa), channel_id=1, source_target_pairs={{0,8},{4,12},{8,16},{12,20},{16,24},{20,28},{1,9},{5,13},{9,17},{1... | collective-permute-start | bytes 835592 | tf_op jit(solution)/shard_map/ppermute | solution.py:613
  16.6 4.7 %collective-permute-done.3.pb = bf16[272,512]{1,0:T(8,128)(2,1)S(1)} collective-permute-done((bf16[272,512]{1,0:T(8,128)(2,1)S(1)}, bf16[272,512]{1,0:T(8,128)(2,1)S(1)}, u32[]{:S(2)}, u32[]{:S(2)}) %collective-permute-start.3) | collective-permute-done | bytes 278560 | tf_op jit(solution)/shard_map/ppermute | solution.py:585
  21.2 1.3 %collective-permute-start.5 = (bf16[272,512]{1,0:T(8,128)(2,1)S(1)}, bf16[272,512]{1,0:T(8,128)(2,1)S(1)}, u32[]{:S(2)}, u32[]{:S(2)}) collective-permute-start(bf16[272,512]{1,0:T(8,128)(2,1)S(1)} %collective-permute-done.3.pb), channel_id=1, source_target_pairs={{0,8},{4,12},{8,16},{12,20},{16,24},{20,28},{1,9},{5,13},{9,17},{1... | collective-permute-start | bytes 835592 | tf_op jit(solution)/shard_map/ppermute | solution.py:614
  22.5 0.0 collective-permute-done.swap
  22.5 2.8 %shard_map.85 = (bf16[272,512]{1,0:T(8,128)(2,1)S(1)}, bf16[1152,512]{1,0:T(8,128)(2,1)S(1)}, bf16[1152,512]{1,0:T(8,128)(2,1)S(1)}, f32[4,256,128]{2,1,0:T(8,12...) custom-call(bf16[128,512]{1,0:T(8,128)(2,1)S(1)} %get-tuple-element., ...), custom_call_target="tpu_custom_call" | custom-call | flops 1500000000 | bytes 6000000 | tf_op jit(solution)/shard_map/pallas_call | solution.py:642
  25.4 1.3 %collective-permute-start.2 = (bf16[256,512]{1,0:T(8,128)(2,1)S(1)}, bf16[256,512]{1,0:T(8,128)(2,1)S(1)}, u32[]{:S(2)}, u32[]{:S(2)}) collective-permute-start(bf16[256,512]{1,0:T(8,128)(2,1)S(1)} %get-tuple-element.51), channel_id=1, source_target_pairs={{0,24},{4,28},{1,25},{5,29},{2,26},{6,30},{3,27},{7,31}} | collective-permute-start | bytes 786440 | tf_op jit(solution)/shard_map/ppermute | solution.py:653
  26.7 2.8 %shard_map.86 = (bf16[272,512]{1,0:T(8,128)(2,1)S(1)}, bf16[1152,512]{1,0:T(8,128)(2,1)S(1)}, bf16[1152,512]{1,0:T(8,128)(2,1)S(1)}, f32[4,256,128]{2,1,0:T(8,12...) custom-call(bf16[272,512]{1,0:T(8,128)(2,1)S(1)} %collective-permute, ...), custom_call_target="tpu_custom_call", output_to_operand_aliasing={{0}: (5, {}), {1}: (6, {}), {2}: (7, {}), {3}: (8, {}), {4}... | custom-call | flops 1500000000 | bytes 6000000 | tf_op jit(solution)/shard_map/pallas_call | solution.py:654
  29.5 0.0 collective-permute-done.4.fa
  29.5 7.9 %collective-permute-done.5.fb = bf16[272,512]{1,0:T(8,128)(2,1)S(1)} collective-permute-done((bf16[272,512]{1,0:T(8,128)(2,1)S(1)}, bf16[272,512]{1,0:T(8,128)(2,1)S(1)}, u32[]{:S(2)}, u32[]{:S(2)}) %collective-permute-start.5) | collective-permute-done | bytes 278560 | tf_op jit(solution)/shard_map/ppermute | solution.py:614
  37.4 3.0 %shard_map.87 = (bf16[1152,512]{1,0:T(8,128)(2,1)S(1)}, bf16[1152,512]{1,0:T(8,128)(2,1)S(1)}, f32[4,256,128]{2,1,0:T(8,128)S(1)}, f32[4,256,128]{2,1,0:T(8,128)S(1)}, f32[4,256,512]{2,1,0:T(8,128)S(1)}) custom-call(bf16[272,512]{1,0:T(8,128)(2,1)S(1)} %collective-permute-done.4.fa, ...), custom_call_target="tpu_custom_call", output_to_operand_aliasing={{0}: (6, {}), {1}: (7, {}), {2}: (8, {}), {3}: (9, {}), {4}... | custom-call | flops 1500000000 | bytes 6000000 | tf_op jit(solution)/shard_map/pallas_call | solution.py:664
  40.4 0.5 shard_map.88.odd_ref
  40.9 0.0 collective-permute-done.2.last
  40.9 2.3 %shard_map.89 = (bf16[128,512]{1,0:T(8,128)(2,1)S(1)}, bf16[128,512]{1,0:T(8,128)(2,1)S(1)}, bf16[1152,512]{1,0:T(8,128)(2,1)S(1)}, bf16[1152,512]{1,0:T(8,128)(2,1)S(1)}) custom-call(f32[16,128]{1,0:T(8,128)S(1)} %get-tuple-element.43.mix_ref, f32[1,512]{1,0:T(1,128)S(1)} %get-tuple-element.44.gain_ref, ...), custom_call_target="tpu_custom_call", output_to_operand_aliasing={{2}: (8, {}), {3}: (9, {})} | custom-call | flops 750000000 | bytes 3000000 | tf_op jit(solution)/shard_map/pallas_call | solution.py:685
  43.2 0.6 collective-permute-start.6
  43.8 0.7 %shard_map.90.part_ref = f32[4,128,1024]{2,1,0:T(8,128)S(1)} custom-call(bf16[128,512]{1,0:T(8,128)(2,1)S(1)} %get-tuple-element.75.x_ref, bf16[4,512,1024]{2,1,0:T(8,128)(2,1)S(1)} %get-tuple-element.76.w_ref), custom_call_target="tpu_custom_call" | custom-call | flops 536870912 | bytes 8000000 | tf_op jit(solution)/shard_map/pallas_call | solution.py:697
  44.5 3.7 %collective-permute-done.6.x_ref = bf16[128,512]{1,0:T(8,128)(2,1)S(1)} collective-permute-done((bf16[128,512]{1,0:T(8,128)(2,1)S(1)}, bf16[128,512]{1,0:T(8,128)(2,1)S(1)}, u32[]{:S(2)}, u32[]{:S(2)}) %collective-permute-start.6) | collective-permute-done | bytes 131104 | tf_op jit(solution)/shard_map/ppermute | solution.py:695
  48.2 0.5 shard_map.92
  48.7 0.1 collective-permute-start.8
  48.8 0.5 shard_map.91
  49.2 0.6 collective-permute-start.7
  49.8 0.5 collective-permute-done.8
  50.3 0.1 add_convert_fusion.1
  50.4 0.6 collective-permute-start.9
  50.9 0.0 collective-permute-done.7
  51.0 7.8 %collective-permute-done.9 = bf16[128,1024]{1,0:T(8,128)(2,1)S(1)} collective-permute-done((bf16[128,1024]{1,0:T(8,128)(2,1)S(1)}, bf16[128,1024]{1,0:T(8,128)(2,1)S(1)}, u32[]{:S(2)}, u32[]{:S(2)}) %collective-permute-start.9) | collective-permute-done | bytes 262176 | tf_op jit(solution)/shard_map/ppermute | solution.py:724
  58.8 0.8 %add_convert_fusion = bf16[128,1024]{1,0:T(8,128)(2,1)} fusion(bf16[128,1024]{1,0:T(8,128)(2,1)S(1)} %collective-permute-done.9, bf16[128,1024]{1,0:T(8,128)(2,1)S(1)} %collective-permute-done.7, bf16[128,1024]{1,0:T(8,128)(2,1)S(1)} %get-tuple-element.77), kind=kLoop, calls=%fused_computation | loop fusion | flops 786432 | bytes 1048576 | tf_op jit(solution)/shard_map/convert_element_type | solution.py:728
Async XLA Ops:
  1.3 21.2 %collective-permute-start = (bf16[384,512]{1,0:T(8,128)(2,1)S(1)}, bf16[384,512]{1,0:T(8,128)(2,1)S(1)}, u32[]{:S(2)}, u32[]{:S(2)}) collective-permute-start(bf16[384,512]{1,0:T(8,128)(2,1)S(1)} %get-tuple-element.46), channel_id=1, source_target_pairs={{0,4},{4,0},{8,12},{12,8},{16,20},{20,16},{24,28},{28,24},{1,5},{5... | collective-permute-start | bytes 1179656 | tf_op jit(solution)/shard_map/ppermute | solution.py:586
  3.8 11.4 %collective-permute-start.1 = (bf16[272,512]{1,0:T(8,128)(2,1)S(1)}, bf16[272,512]{1,0:T(8,128)(2,1)S(1)}, u32[]{:S(2)}, u32[]{:S(2)}) collective-permute-start(bf16[272,512]{1,0:T(8,128)(2,1)S(1)} %shard_map.84.own_kv), channel_id=1, source_target_pairs={{0,8},{4,12},{8,16},{12,20},{16,24},{20,28},{1,9},{5,13},{9,17},{1... | collective-permute-start | bytes 835592 | tf_op jit(solution)/shard_map/ppermute | solution.py:584
  5.1 16.1 %collective-permute-start.3 = (bf16[272,512]{1,0:T(8,128)(2,1)S(1)}, bf16[272,512]{1,0:T(8,128)(2,1)S(1)}, u32[]{:S(2)}, u32[]{:S(2)}) collective-permute-start(bf16[272,512]{1,0:T(8,128)(2,1)S(1)} %get-tuple-element.53), channel_id=1, source_target_pairs={{0,12},{4,8},{8,20},{12,16},{16,28},{20,24},{1,13},{5,9},{9,21},{1... | collective-permute-start | bytes 835592 | tf_op jit(solution)/shard_map/ppermute | solution.py:585
  15.3 14.2 %collective-permute-start.4 = (bf16[272,512]{1,0:T(8,128)(2,1)S(1)}, bf16[272,512]{1,0:T(8,128)(2,1)S(1)}, u32[]{:S(2)}, u32[]{:S(2)}) collective-permute-start(bf16[272,512]{1,0:T(8,128)(2,1)S(1)} %collective-permute-done.1.pa), channel_id=1, source_target_pairs={{0,8},{4,12},{8,16},{12,20},{16,24},{20,28},{1,9},{5,13},{9,17},{1... | collective-permute-start | bytes 835592 | tf_op jit(solution)/shard_map/ppermute | solution.py:613
  21.2 16.2 %collective-permute-start.5 = (bf16[272,512]{1,0:T(8,128)(2,1)S(1)}, bf16[272,512]{1,0:T(8,128)(2,1)S(1)}, u32[]{:S(2)}, u32[]{:S(2)}) collective-permute-start(bf16[272,512]{1,0:T(8,128)(2,1)S(1)} %collective-permute-done.3.pb), channel_id=1, source_target_pairs={{0,8},{4,12},{8,16},{12,20},{16,24},{20,28},{1,9},{5,13},{9,17},{1... | collective-permute-start | bytes 835592 | tf_op jit(solution)/shard_map/ppermute | solution.py:614
  25.4 15.6 %collective-permute-start.2 = (bf16[256,512]{1,0:T(8,128)(2,1)S(1)}, bf16[256,512]{1,0:T(8,128)(2,1)S(1)}, u32[]{:S(2)}, u32[]{:S(2)}) collective-permute-start(bf16[256,512]{1,0:T(8,128)(2,1)S(1)} %get-tuple-element.51), channel_id=1, source_target_pairs={{0,24},{4,28},{1,25},{5,29},{2,26},{6,30},{3,27},{7,31}} | collective-permute-start | bytes 786440 | tf_op jit(solution)/shard_map/ppermute | solution.py:653
  43.2 5.0 %collective-permute-start.6 = (bf16[128,512]{1,0:T(8,128)(2,1)S(1)}, bf16[128,512]{1,0:T(8,128)(2,1)S(1)}, u32[]{:S(2)}, u32[]{:S(2)}) collective-permute-start(bf16[128,512]{1,0:T(8,128)(2,1)S(1)} %get-tuple-element.73), channel_id=1, source_target_pairs={{0,4},{4,0},{8,12},{12,8},{16,20},{20,16},{24,28},{28,24},{1,5},{5... | collective-permute-start | bytes 393224 | tf_op jit(solution)/shard_map/ppermute | solution.py:695
  48.7 1.6 %collective-permute-start.8 = (bf16[128,1024]{1,0:T(8,128)(2,1)S(1)}, bf16[128,1024]{1,0:T(8,128)(2,1)S(1)}, u32[]{:S(2)}, u32[]{:S(2)}) collective-permute-start(bf16[128,1024]{1,0:T(8,128)(2,1)S(1)} %get-tuple-element.80), channel_id=1, source_target_pairs={{0,1},{1,0},{2,3},{3,2},{4,5},{5,4},{6,7},{7,6},{8,9},{9,8},{10,11... | collective-permute-start | bytes 786440 | tf_op jit(solution)/shard_map/ppermute | solution.py:722
  49.2 1.7 %collective-permute-start.7 = (bf16[128,1024]{1,0:T(8,128)(2,1)S(1)}, bf16[128,1024]{1,0:T(8,128)(2,1)S(1)}, u32[]{:S(2)}, u32[]{:S(2)}) collective-permute-start(bf16[128,1024]{1,0:T(8,128)(2,1)S(1)} %get-tuple-element.78), channel_id=1, source_target_pairs={{0,1},{1,0},{2,3},{3,2},{4,5},{5,4},{6,7},{7,6},{8,9},{9,8},{10,11... | collective-permute-start | bytes 786440 | tf_op jit(solution)/shard_map/ppermute | solution.py:726
  50.4 8.4 %collective-permute-start.9 = (bf16[128,1024]{1,0:T(8,128)(2,1)S(1)}, bf16[128,1024]{1,0:T(8,128)(2,1)S(1)}, u32[]{:S(2)}, u32[]{:S(2)}) collective-permute-start(bf16[128,1024]{1,0:T(8,128)(2,1)S(1)} %add_convert_fusion.1), channel_id=1, source_target_pairs={{0,2},{1,3},{2,0},{3,1},{4,6},{5,7},{6,4},{7,5},{8,10},{9,11},{10,... | collective-permute-start | bytes 786440 | tf_op jit(solution)/shard_map/ppermute | solution.py:724
where the time goes:
time: 59.9 us; the launch traced here: 59.6 us
  waiting for transfers between devices  30.1 us (50%)
  Pallas kernels  18.7 us (31%)
  starting transfers between devices  9.78 us (16%)
  other arithmetic  0.89 us (1%)
    ppermute x1, waiting for transfers between devices, paired_plan(): fb = lax.ppermute(pbk, 'pb', up)  7.86 us
    ppermute x1, waiting for transfers between devices, paired_plan(): arrived = lax.ppermute(away, 'ha', [(i, i ^ 2) for i in range(n_ha)])  7.82 us
    ppermute x1, waiting for transfers between devices, paired_plan(): pa = lax.ppermute(own_kv, 'pb', up)  5.47 us
    ppermute x1, waiting for transfers between devices, paired_plan(): pbk = lax.ppermute(oth_kv, 'pb', cross)  4.65 us
    ppermute x1, waiting for transfers between devices, paired_plan(): got = lax.ppermute(theirs, 'pb', swap_route)  3.72 us
    pallas_call x1, Pallas kernels, paired_plan(): pl.pallas_call(functools.partial(prep_kernel, scale=1.0 / math.sqrt(dh)),...  3.35 us
    pallas_call x1, Pallas kernels, paired_plan(): pl.pallas_call(mid_kernel, out_shape=(span, span) + state(on_chip), in_sp...  3 us
    pallas_call x1, Pallas kernels, paired_plan(): pl.pallas_call(own_kernel, out_shape=(on_chip((n_ext, half), bf), span, s...  2.85 us
  transfers between devices with their start and end apart: 10, of which 6 were waited for; matrix products, arithmetic and copies ran while one was open for 0% of the time, Pallas kernels for 25%

commit v1 on v0

--- a/solution.py
+++ b/solution.py
@@ -16,6 +16,7 @@
 HALO = 16
 NEG = -1e30
 FLOOR = -5e29
+INSET = 16
 
 
 def place():
@@ -92,8 +93,8 @@
             tap = 2 * q + side
             for b in range(-reach, reach + 1):
                 t = theta_ref[tap, base + h, b + reach] * scale
-                lo = jnp.where(diff == b - 64, t, lo)
-                hi = jnp.where(diff == b + 64, t, hi)
+                lo = jnp.where(diff == b - INSET, t, lo)
+                hi = jnp.where(diff == b + width - INSET, t, hi)
             w_ref[step, 0:width, side * width : (side + 1) * width] = lo.astype(jnp.bfloat16)
             w_ref[step, width : 2 * width, side * width : (side + 1) * width] = hi.astype(
                 jnp.bfloat16
@@ -131,13 +132,13 @@
         ok = (col >= start_ext) & (col <= row_ext)
         score_ok[t] = jnp.where(ok, 1.0, 0.0)
     for t in range(2):
-        col = col0 + 64 + t * 128 + lane
+        col = col0 + INSET + t * 128 + lane
         ok = (col >= start_ext[HALO:]) & (col <= row_ext[HALO:])
         bias[t] = jnp.where(ok, 0.0, NEG)
 
 
 def reaches(start, row0, col0):
-    return jnp.min(start[row0 + HALO : row0 + HALO + 8, :]) < col0 + 64 + 256
+    return jnp.min(start[row0 + HALO : row0 + HALO + 8, :]) < col0 + INSET + 256
 
 
 def one_window(at, row0, n_rows, qs, ks, vs, w, same, work, state, result):
@@ -159,7 +160,8 @@
             preferred_element_type=jnp.float32,
         )
         for t in range(3):
-            piece = (s[:, t * 128 : (t + 1) * 128] * score_ok[t]).astype(jnp.bfloat16)
+            piece = jnp.where(score_ok[t] > 0.0, s[:, t * 128 : (t + 1) * 128], 0.0)
+            piece = piece.astype(jnp.bfloat16)
             if t < 2:
                 lhs[buf, 0:n_ext, t * 128 : (t + 1) * 128] = piece
             if t > 0:
@@ -174,13 +176,13 @@
     def weigh(h, r):
         buf = h % 2
         rows = pl.ds(row0 + r, step)
-        keep = [same[a - 1, rows, :] for a in range(1, QCONV)]
+        keep = [same[a - 1, rows, :] > 0.0 for a in range(1, QCONV)]
         parts = []
         for t in range(2):
             base = t * n_ext + HALO + r
             conv = ps[buf, 0, base : base + step, :] + bias[t, r : r + step, :]
             for a in range(1, QCONV):
-                conv = conv + ps[buf, a, base - a : base - a + step, :] * keep[a - 1]
+                conv = conv + jnp.where(keep[a - 1], ps[buf, a, base - a : base - a + step, :], 0.0)
             parts.append(conv)
         old = peak[h, rows, :]
         top = jnp.max(jnp.maximum(parts[0], parts[1]), axis=1, keepdims=True)
@@ -201,7 +203,7 @@
         buf = h % 2
         out_rows = pl.ds(row0, n_rows) if peak_out is not None else pl.ds(0, n_rows)
         upd = jnp.dot(
-            probs[buf], vs[pl.ds(at + 64, 256), :], preferred_element_type=jnp.float32
+            probs[buf], vs[pl.ds(at + INSET, 256), :], preferred_element_type=jnp.float32
         )
         factor = factors[buf]
         for t in range(GROUP):
@@ -231,7 +233,7 @@
     vs[at, :] = src[lo + rows : lo + 2 * rows, :]
 
 
-def load_weights(out_weight, dst, who, sems):
+def load_weights(out_weight, dst, who, sems, skip=0):
     half, part = dst.shape[1:]
     ha = lax.axis_index("ha")
     core = lax.rem(ha, 2)
@@ -241,34 +243,37 @@
     copies = []
     for n in range(dst.shape[0]):
         rows = pl.ds(pl.multiple_of(who * half, half), half)
-        cols = pl.ds(pl.multiple_of(order[n] * part, part), part)
+        cols = pl.ds(pl.multiple_of(order[skip + n] * part, part), part)
         copy = pltpu.make_async_copy(out_weight.at[rows, cols], dst.at[n], sems.at[n])
         copy.start()
         copies.append(copy)
     return copies
 
 
+def far_source_kernel(own_kv, swap, out_ref):
+    side, _ = place()
+    rows = out_ref.shape[0] // 2
+
+    @pl.when(side == 0)
+    def _():
+        out_ref[...] = swap[rows : 3 * rows, :]
+
+    @pl.when(side == 1)
+    def _():
+        out_ref[...] = own_kv[HALO : HALO + 2 * rows, :]
+
+
 def own_kernel(
-    own_q, own_kv, swap, out_weight, w, start, same,
-    qs, ks, vs, peak, total, acc, w_oth, e_src, score_ok, bias, lhs, ps, probs, factors, sems
+    own_q, own_kv, swap, w, start, same,
+    qs, ks, vs, peak, total, acc, score_ok, bias, lhs, ps, probs, factors
 ):
     rows, half = own_q.shape
     side, first = place()
     first_row = first * rows
-    copies = load_weights(out_weight, w_oth, 1 - side, sems)
     qs[pl.ds(pl.multiple_of(HALO + side * rows, HALO), rows), :] = own_q[...]
     qs[pl.ds(pl.multiple_of(HALO + (1 - side) * rows, HALO), rows), :] = swap[0:rows, :]
 
     qs[0:HALO, :] = jnp.zeros((HALO, half), jnp.bfloat16)
-
-    @pl.when(side == 0)
-    def _():
-        e_src[...] = swap[rows : 3 * rows, :]
-
-    @pl.when(side == 1)
-    def _():
-        e_src[...] = own_kv[HALO : HALO + 2 * rows, :]
-
     zero = jnp.zeros((rows, half), jnp.bfloat16)
     for blk in (0, 1, 8):
         ks[blk * rows : (blk + 1) * rows, :] = zero
@@ -284,8 +289,6 @@
         6 * rows, 0, 2 * rows, qs, ks, vs, w, same,
         (score_ok, bias, lhs, ps, probs, factors), state, state,
     )
-    for copy in copies:
-        copy.wait()
 
 
 def next_kernel(
@@ -321,8 +324,8 @@
     rows = (qs.shape[0] - HALO) // 2
     side, first = place()
     first_row = first * rows
-    put(fa, HALO, ks, vs, 2 + side)
-    put(fb, HALO, ks, vs, 3 - side)
+    put(fa, 0, ks, vs, 2 + side)
+    put(fb, 0, ks, vs, 3 - side)
     state = (peak, total, acc)
 
     @pl.when(reaches(start, 0, first_row - 4 * rows))
@@ -403,14 +406,25 @@
         theirs_ref[...] = even_ref[...]
 
 
-def own_part_kernel(x_ref, w_ref, out_ref):
+def own_part_kernel(x_ref, w_ref, out_weight, out_ref, w_far, sems):
+    side, _ = place()
+    copies = load_weights(out_weight, w_far, 1 - side, sems)
     for n in range(w_ref.shape[0]):
         out_ref[n] = jnp.dot(x_ref[...], w_ref[n], preferred_element_type=jnp.float32)
+    for copy in copies:
+        copy.wait()
+
+
+def late_part_kernel(x_ref, out_weight, part_ref, give_ref, keep_ref, w_near, sems):
+    side, _ = place()
+    for copy in load_weights(out_weight, w_near, 1 - side, sems, skip=2):
+        copy.wait()
+    add_part_kernel(x_ref, w_near, part_ref, give_ref, keep_ref, lo=2)
 
 
 def add_part_kernel(x_ref, w_ref, part_ref, give_ref, keep_ref, *, lo):
     for n, out_ref in enumerate((give_ref, keep_ref)):
-        out = jnp.dot(x_ref[...], w_ref[lo + n], preferred_element_type=jnp.float32)
+        out = jnp.dot(x_ref[...], w_ref[n], preferred_element_type=jnp.float32)
         out_ref[...] = (out + part_ref[lo + n]).astype(jnp.bfloat16)
 
 
@@ -610,8 +624,8 @@
         ),
     )(stay(turn_lengths), stay(theta.transpose(1, 0, 2)), stay(mix.T), stay(gain.reshape(1, -1)), heavy)
     pa, w = lax.optimization_barrier((pa, w))
-    fa = lax.ppermute(pa, "pb", up)
-    fb = lax.ppermute(pbk, "pb", up)
+    fa = lax.ppermute(pa[HALO:], "pb", up)
+    fb = lax.ppermute(pbk[HALO:], "pb", up)
 
     def state(make):
         return (
@@ -638,19 +652,27 @@
             transcendentals=int(n * 300_000),
         )
 
+    some_weights = on_chip((2, half, part), bf)
     span = on_chip((9 * rows, half), bf)
-    qs, ks, vs, peak, total, acc, w_oth, e_src = pl.pallas_call(
+    e_src = pl.pallas_call(
+        far_source_kernel,
+        out_shape=on_chip((2 * rows, half), bf),
+        in_specs=[vm, vm],
+        out_specs=vm,
+        compiler_params=small,
+    )(own_kv, swap)
+    last = lax.ppermute(e_src, "pb", far)
+    qs, ks, vs, peak, total, acc = pl.pallas_call(
         own_kernel,
         out_shape=(on_chip((n_ext, half), bf), span, span)
         + state(on_chip)
-        + (weights, on_chip((2 * rows, half), bf)),
-        in_specs=[vm] * 3 + [hbm] + [vm] * 3,
-        out_specs=(vm,) * 8,
-        scratch_shapes=work(n_rows) + [pltpu.SemaphoreType.DMA((n_ha,))],
+,
+        in_specs=[vm] * 6,
+        out_specs=(vm,) * 6,
+        scratch_shapes=work(n_rows),
         compiler_params=params,
         cost_estimate=cost(1),
-    )(own_q, own_kv, swap, heavy, w, start, same)
-    last = lax.ppermute(e_src, "pb", far)
+    )(own_q, own_kv, swap, w, start, same)
     qs, ks, vs, peak, total, acc = pl.pallas_call(
         next_kernel,
         out_shape=(on_chip((n_ext, half), bf), span, span) + state(on_chip),
@@ -694,35 +716,43 @@
     )(blend, gain_own, odd, last, w, start, same, qs, ks, vs, peak, total, acc)
     got = lax.ppermute(theirs, "pb", swap_route)
 
-    own_part = pl.pallas_call(
+    own_part, w_far = pl.pallas_call(
         own_part_kernel,
-        out_shape=on_chip((n_ha, rows, part), f32),
-        in_specs=[vm, vm],
-        out_specs=vm,
+        out_shape=(on_chip((n_ha, rows, part), f32), some_weights),
+        in_specs=[vm, vm, hbm],
+        out_specs=(vm, vm),
+        scratch_shapes=[pltpu.SemaphoreType.DMA((2,))],
         compiler_params=params,
         cost_estimate=pl.CostEstimate(
             flops=2 * rows * half * cols, bytes_accessed=8_000_000, transcendentals=0
         ),
-    )(mine, w_own)
-
-    def finish(lo, got):
-        return pl.pallas_call(
-            functools.partial(add_part_kernel, lo=lo),
-            out_shape=(on_chip((rows, part), bf), on_chip((rows, part), bf)),
-            in_specs=[vm, vm, vm],
-            out_specs=(vm, vm),
-            compiler_params=params,
-            cost_estimate=pl.CostEstimate(
-                flops=rows * half * cols, bytes_accessed=4_000_000, transcendentals=0
-            ),
-        )(got, w_oth, own_part)
+    )(mine, w_own, heavy)
+    halves = (on_chip((rows, part), bf), on_chip((rows, part), bf))
+    half_cost = pl.CostEstimate(
+        flops=rows * half * cols, bytes_accessed=4_000_000, transcendentals=0
+    )
 
     near_route = [(i, i ^ 1) for i in range(n_ha)]
-    give, keep = finish(0, got)
+    give, keep = pl.pallas_call(
+        functools.partial(add_part_kernel, lo=0),
+        out_shape=halves,
+        in_specs=[vm, vm, vm],
+        out_specs=(vm, vm),
+        compiler_params=params,
+        cost_estimate=half_cost,
+    )(got, w_far, own_part)
     take = lax.ppermute(give, "ha", near_route)
     away = (keep.astype(f32) + take.astype(f32)).astype(bf)
     arrived = lax.ppermute(away, "ha", [(i, i ^ 2) for i in range(n_ha)])
-    give, keep = finish(2, got)
+    give, keep = pl.pallas_call(
+        late_part_kernel,
+        out_shape=halves,
+        in_specs=[vm, hbm, vm],
+        out_specs=(vm, vm),
+        scratch_shapes=[pltpu.VMEM((2, half, part), bf), pltpu.SemaphoreType.DMA((2,))],
+        compiler_params=params,
+        cost_estimate=half_cost,
+    )(got, heavy, own_part)
     take = lax.ppermute(give, "ha", near_route)
     here = keep.astype(f32) + take.astype(f32)
     return (here + arrived.astype(f32)).astype(bf)

time: 59.9 us -> 60.2 us (level)
  the two profiles are of different devices: /device:TPU:28 before, /device:TPU:24 now
where the time goes in v1:
time: 60.2 us; the launch traced here: 59.8 us
  waiting for transfers between devices  26.2 us (44%)
  Pallas kernels  21.7 us (36%)
  starting transfers between devices  10.8 us (18%)
  other arithmetic  0.89 us (1%)
    ppermute x1, waiting for transfers between devices, paired_plan(): fb = lax.ppermute(pbk[HALO:], 'pb', up)  7.17 us
    ppermute x1, waiting for transfers between devices, paired_plan(): arrived = lax.ppermute(away, 'ha', [(i, i ^ 2) for i in range(n_ha)])  6.72 us
    ppermute x1, waiting for transfers between devices, paired_plan(): pa = lax.ppermute(own_kv, 'pb', up)  5.47 us
    ppermute x1, waiting for transfers between devices, paired_plan(): pbk = lax.ppermute(oth_kv, 'pb', cross)  4.62 us
    pallas_call x1, Pallas kernels, paired_plan(): pl.pallas_call(functools.partial(prep_kernel, scale=1.0 / math.sqrt(dh)),...  3.35 us
    pallas_call x1, Pallas kernels, paired_plan(): pl.pallas_call(mid_kernel, out_shape=(span, span) + state(on_chip), in_sp...  2.97 us
    pallas_call x1, Pallas kernels, paired_plan(): pl.pallas_call(next_kernel, out_shape=(on_chip((n_ext, half), bf), span,...  2.82 us
    pallas_call x1, Pallas kernels, paired_plan(): pl.pallas_call(own_kernel, out_shape=(on_chip((n_ext, half), bf), span, s...  2.78 us
  transfers between devices with their start and end apart: 10, of which 5 were waited for; matrix products, arithmetic and copies ran while one was open for 0% of the time, Pallas kernels for 30%

profile of v1, /device:TPU:24, one launch (start us, length us, event | category | flops | bytes accessed | tf_op | source)
XLA Modules:
  0.0 59.8 jit_solution(1314332190715315668)
XLA Ops:
  0.0 1.3 %shard_map.84 = (bf16[128,512]{1,0:T(8,128)(2,1)S(1)}, bf16[384,512]{1,0:T(8,128)(2,1)S(1)}, bf16[272,512]{1,0:T(8,128)(2,1)S(1)}) custom-call(bf16[128,1024]{1,0:T(8,128)(2,1)} %q_ref.3, bf16[128,1024]{1,0:T(8,128)(2,1)} %k_ref.3, bf16[128,1024]{1,0:T(8,128)(2,1)} %v_ref.3), custom_call_target="tpu_custom_call" | custom-call | tf_op jit(solution)/shard_map/pallas_call | solution.py:579
  1.3 1.6 %collective-permute-start = (bf16[384,512]{1,0:T(8,128)(2,1)S(1)}, bf16[384,512]{1,0:T(8,128)(2,1)S(1)}, u32[]{:S(2)}, u32[]{:S(2)}) collective-permute-start(bf16[384,512]{1,0:T(8,128)(2,1)S(1)} %get-tuple-element.45), channel_id=1, source_target_pairs={{0,4},{4,0},{8,12},{12,8},{16,20},{20,16},{24,28},{28,24},{1,5},{5... | collective-permute-start | bytes 1179656 | tf_op jit(solution)/shard_map/ppermute | solution.py:600
  2.8 1.0 %shard_map.83.own_kv = bf16[272,512]{1,0:T(8,128)(2,1)S(1)} custom-call(bf16[128,1024]{1,0:T(8,128)(2,1)} %q_ref.3, bf16[128,1024]{1,0:T(8,128)(2,1)} %k_ref.3, bf16[128,1024]{1,0:T(8,128)(2,1)} %v_ref.3), custom_call_target="tpu_custom_call" | custom-call | tf_op jit(solution)/shard_map/pallas_call | solution.py:571
  3.8 1.3 %collective-permute-start.2 = (bf16[272,512]{1,0:T(8,128)(2,1)S(1)}, bf16[272,512]{1,0:T(8,128)(2,1)S(1)}, u32[]{:S(2)}, u32[]{:S(2)}) collective-permute-start(bf16[272,512]{1,0:T(8,128)(2,1)S(1)} %shard_map.83.own_kv), channel_id=1, source_target_pairs={{0,8},{4,12},{8,16},{12,20},{16,24},{20,28},{1,9},{5,13},{9,17},{1... | collective-permute-start | bytes 835592 | tf_op jit(solution)/shard_map/ppermute | solution.py:598
  5.1 1.3 %collective-permute-start.3 = (bf16[272,512]{1,0:T(8,128)(2,1)S(1)}, bf16[272,512]{1,0:T(8,128)(2,1)S(1)}, u32[]{:S(2)}, u32[]{:S(2)}) collective-permute-start(bf16[272,512]{1,0:T(8,128)(2,1)S(1)} %get-tuple-element.51), channel_id=1, source_target_pairs={{0,12},{4,8},{8,20},{12,16},{16,28},{20,24},{1,13},{5,9},{9,21},{1... | collective-permute-start | bytes 835592 | tf_op jit(solution)/shard_map/ppermute | solution.py:599
  6.4 3.3 %shard_map.82 = (bf16[12,256,256]{2,1,0:T(8,128)(2,1)S(1)}, s32[272,128]{1,0:T(8,128)S(1)}, f32[5,256,128]{2,1,0:T(8,128)S(1)}, bf16[4,512,1024]{2,1,0:T(8,128)(...) custom-call(s32[16]{0:T(128)} %len_ref.1, f32[6,8,11]{2,1,0:T(8,128)} %bitcast.3, f32[4,8]{1,0:T(4,128)} %bitcast.5, ...), custom_call_target="tpu_custom_call" | custom-call | flops 20000000 | bytes 2400000 | tf_op jit(solution)/shard_map/pallas_call | solution.py:608
  9.8 5.5 %collective-permute-done.2.pa = bf16[272,512]{1,0:T(8,128)(2,1)S(1)} collective-permute-done((bf16[272,512]{1,0:T(8,128)(2,1)S(1)}, bf16[272,512]{1,0:T(8,128)(2,1)S(1)}, u32[]{:S(2)}, u32[]{:S(2)}) %collective-permute-start.2) | collective-permute-done | bytes 278560 | tf_op jit(solution)/shard_map/ppermute | solution.py:598
  15.3 1.3 %collective-permute-start.4 = (bf16[256,512]{1,0:T(8,128)(2,1)S(1)}, bf16[256,512]{1,0:T(8,128)(2,1)S(1)}, u32[]{:S(2)}, u32[]{:S(2)}) collective-permute-start(bf16[256,512]{1,0:T(8,128)(2,1)S(1)} %slice.6), channel_id=1, source_target_pairs={{0,8},{4,12},{8,16},{12,20},{16,24},{20,28},{1,9},{5,13},{9,17},{1... | collective-permute-start | bytes 786440 | tf_op jit(solution)/shard_map/ppermute | solution.py:627
  16.6 4.6 %collective-permute-done.3.pb = bf16[272,512]{1,0:T(8,128)(2,1)S(1)} collective-permute-done((bf16[272,512]{1,0:T(8,128)(2,1)S(1)}, bf16[272,512]{1,0:T(8,128)(2,1)S(1)}, u32[]{:S(2)}, u32[]{:S(2)}) %collective-permute-start.3) | collective-permute-done | bytes 278560 | tf_op jit(solution)/shard_map/ppermute | solution.py:599
  21.2 1.3 %collective-permute-start.5 = (bf16[256,512]{1,0:T(8,128)(2,1)S(1)}, bf16[256,512]{1,0:T(8,128)(2,1)S(1)}, u32[]{:S(2)}, u32[]{:S(2)}) collective-permute-start(bf16[256,512]{1,0:T(8,128)(2,1)S(1)} %slice.8), channel_id=1, source_target_pairs={{0,8},{4,12},{8,16},{12,20},{16,24},{20,28},{1,9},{5,13},{9,17},{1... | collective-permute-start | bytes 786440 | tf_op jit(solution)/shard_map/ppermute | solution.py:628
  22.5 0.0 collective-permute-done.swap
  22.6 1.3 %collective-permute-start.1 = (bf16[256,512]{1,0:T(8,128)(2,1)S(1)}, bf16[256,512]{1,0:T(8,128)(2,1)S(1)}, u32[]{:S(2)}, u32[]{:S(2)}) collective-permute-start(bf16[256,512]{1,0:T(8,128)(2,1)S(1)} %shard_map.85), channel_id=1, source_target_pairs={{0,24},{4,28},{1,25},{5,29},{2,26},{6,30},{3,27},{7,31}} | collective-permute-start | bytes 786440 | tf_op jit(solution)/shard_map/ppermute | solution.py:664
  23.9 2.8 %shard_map.86 = (bf16[272,512]{1,0:T(8,128)(2,1)S(1)}, bf16[1152,512]{1,0:T(8,128)(2,1)S(1)}, bf16[1152,512]{1,0:T(8,128)(2,1)S(1)}, f32[4,256,128]{2,1,0:T(8,12...) custom-call(bf16[128,512]{1,0:T(8,128)(2,1)S(1)} %get-tuple-element.52.own_q, ...), custom_call_target="tpu_custom_call" | custom-call | flops 1500000000 | bytes 6000000 | tf_op jit(solution)/shard_map/pallas_call | solution.py:665
  26.7 2.8 %shard_map.87 = (bf16[272,512]{1,0:T(8,128)(2,1)S(1)}, bf16[1152,512]{1,0:T(8,128)(2,1)S(1)}, bf16[1152,512]{1,0:T(8,128)(2,1)S(1)}, f32[4,256,128]{2,1,0:T(8,12...) custom-call(bf16[272,512]{1,0:T(8,128)(2,1)S(1)} %collective-permute, ...), custom_call_target="tpu_custom_call", output_to_operand_aliasing={{0}: (5, {}), {1}: (6, {}), {2}: (7, {}), {3}: (8, {}), {4}... | custom-call | flops 1500000000 | bytes 6000000 | tf_op jit(solution)/shard_map/pallas_call | solution.py:676
  29.5 0.0 collective-permute-done.4.fa
  29.5 7.2 %collective-permute-done.5.fb = bf16[256,512]{1,0:T(8,128)(2,1)S(1)} collective-permute-done((bf16[256,512]{1,0:T(8,128)(2,1)S(1)}, bf16[256,512]{1,0:T(8,128)(2,1)S(1)}, u32[]{:S(2)}, u32[]{:S(2)}) %collective-permute-start.5) | collective-permute-done | bytes 262176 | tf_op jit(solution)/shard_map/ppermute | solution.py:628
  36.7 3.0 %shard_map.88 = (bf16[1152,512]{1,0:T(8,128)(2,1)S(1)}, bf16[1152,512]{1,0:T(8,128)(2,1)S(1)}, f32[4,256,128]{2,1,0:T(8,128)S(1)}, f32[4,256,128]{2,1,0:T(8,128)S(1)}, f32[4,256,512]{2,1,0:T(8,128)S(1)}) custom-call(bf16[256,512]{1,0:T(8,128)(2,1)S(1)} %collective-permute-done.4.fa, ...), custom_call_target="tpu_custom_call", output_to_operand_aliasing={{0}: (6, {}), {1}: (7, {}), {2}: (8, {}), {3}: (9, {}), {4}... | custom-call | flops 1500000000 | bytes 6000000 | tf_op jit(solution)/shard_map/pallas_call | solution.py:686
  39.7 0.5 shard_map.89.odd_ref
  40.2 0.0 collective-permute-done.1.last
  40.2 2.3 %shard_map.90 = (bf16[128,512]{1,0:T(8,128)(2,1)S(1)}, bf16[128,512]{1,0:T(8,128)(2,1)S(1)}, bf16[1152,512]{1,0:T(8,128)(2,1)S(1)}, bf16[1152,512]{1,0:T(8,128)(2,1)S(1)}) custom-call(f32[16,128]{1,0:T(8,128)S(1)} %get-tuple-element.43.mix_ref, f32[1,512]{1,0:T(1,128)S(1)} %get-tuple-element.44.gain_ref, ...), custom_call_target="tpu_custom_call", output_to_operand_aliasing={{2}: (8, {}), {3}: (9, {})} | custom-call | flops 750000000 | bytes 3000000 | tf_op jit(solution)/shard_map/pallas_call | solution.py:707
  42.5 0.6 %collective-permute-start.6 = (bf16[128,512]{1,0:T(8,128)(2,1)S(1)}, bf16[128,512]{1,0:T(8,128)(2,1)S(1)}, u32[]{:S(2)}, u32[]{:S(2)}) collective-permute-start(bf16[128,512]{1,0:T(8,128)(2,1)S(1)} %get-tuple-element.72), channel_id=1, source_target_pairs={{0,4},{4,0},{8,12},{12,8},{16,20},{20,16},{24,28},{28,24},{1,5},{5... | collective-permute-start | bytes 393224 | tf_op jit(solution)/shard_map/ppermute | solution.py:717
  43.1 2.2 %shard_map.91 = (f32[4,128,1024]{2,1,0:T(8,128)S(1)}, bf16[2,512,1024]{2,1,0:T(8,128)(2,1)S(1)}) custom-call(bf16[128,512]{1,0:T(8,128)(2,1)S(1)} %get-tuple-element.73.x_ref, bf16[4,512,1024]{2,1,0:T(8,128)(2,1)S(1)} %get-tuple-element.74.w_ref, bf16[1024,4096]{1,0:T(8,128)(2,1)} %out_weight.5), custom_call_target="tpu_custom_call" | custom-call | flops 536870912 | bytes 8000000 | tf_op jit(solution)/shard_map/pallas_call | solution.py:719
  45.3 2.2 %collective-permute-done.6.x_ref = bf16[128,512]{1,0:T(8,128)(2,1)S(1)} collective-permute-done((bf16[128,512]{1,0:T(8,128)(2,1)S(1)}, bf16[128,512]{1,0:T(8,128)(2,1)S(1)}, u32[]{:S(2)}, u32[]{:S(2)}) %collective-permute-start.6) | collective-permute-done | bytes 131104 | tf_op jit(solution)/shard_map/ppermute | solution.py:717
  47.5 0.5 shard_map.93
  48.0 0.1 collective-permute-start.8
  48.1 2.0 %shard_map.92 = (bf16[128,1024]{1,0:T(8,128)(2,1)S(1)}, bf16[128,1024]{1,0:T(8,128)(2,1)S(1)}) custom-call(bf16[128,512]{1,0:T(8,128)(2,1)S(1)} %collective-permute-done.6.x_ref, bf16[1024,4096]{1,0:T(8,128)(2,1)} %out_weight.5, f32[4,128,1024]{2,1,0:T(8,128)S(1)} %get-tuple-element.75.part_ref), custom_call_target="tpu_custom_call" | custom-call | flops 268435456 | bytes 4000000 | tf_op jit(solution)/shard_map/pallas_call | solution.py:747
  50.1 0.5 collective-permute-start.7
  50.6 0.0 collective-permute-done.8
  50.6 0.1 add_convert_fusion.1
  50.7 1.6 %collective-permute-start.9 = (bf16[128,1024]{1,0:T(8,128)(2,1)S(1)}, bf16[128,1024]{1,0:T(8,128)(2,1)S(1)}, u32[]{:S(2)}, u32[]{:S(2)}) collective-permute-start(bf16[128,1024]{1,0:T(8,128)(2,1)S(1)} %add_convert_fusion.1), channel_id=1, source_target_pairs={{0,2},{1,3},{2,0},{3,1},{4,6},{5,7},{6,4},{7,5},{8,10},{9,11},{10,... | collective-permute-start | bytes 786440 | tf_op jit(solution)/shard_map/ppermute | solution.py:746
  52.3 0.0 collective-permute-done.7
  52.3 6.7 %collective-permute-done.9 = bf16[128,1024]{1,0:T(8,128)(2,1)S(1)} collective-permute-done((bf16[128,1024]{1,0:T(8,128)(2,1)S(1)}, bf16[128,1024]{1,0:T(8,128)(2,1)S(1)}, u32[]{:S(2)}, u32[]{:S(2)}) %collective-permute-start.9) | collective-permute-done | bytes 262176 | tf_op jit(solution)/shard_map/ppermute | solution.py:746
  59.0 0.8 %add_convert_fusion = bf16[128,1024]{1,0:T(8,128)(2,1)} fusion(bf16[128,1024]{1,0:T(8,128)(2,1)S(1)} %collective-permute-done.9, bf16[128,1024]{1,0:T(8,128)(2,1)S(1)} %collective-permute-done.7, bf16[128,1024]{1,0:T(8,128)(2,1)S(1)} %get-tuple-element.76), kind=kLoop, calls=%fused_computation | loop fusion | flops 786432 | bytes 1048576 | tf_op jit(solution)/shard_map/convert_element_type | solution.py:758
  (3 shorter events, 0.1 us)
Async XLA Ops:
  1.3 21.2 %collective-permute-start = (bf16[384,512]{1,0:T(8,128)(2,1)S(1)}, bf16[384,512]{1,0:T(8,128)(2,1)S(1)}, u32[]{:S(2)}, u32[]{:S(2)}) collective-permute-start(bf16[384,512]{1,0:T(8,128)(2,1)S(1)} %get-tuple-element.45), channel_id=1, source_target_pairs={{0,4},{4,0},{8,12},{12,8},{16,20},{20,16},{24,28},{28,24},{1,5},{5... | collective-permute-start | bytes 1179656 | tf_op jit(solution)/shard_map/ppermute | solution.py:600
  3.8 11.4 %collective-permute-start.2 = (bf16[272,512]{1,0:T(8,128)(2,1)S(1)}, bf16[272,512]{1,0:T(8,128)(2,1)S(1)}, u32[]{:S(2)}, u32[]{:S(2)}) collective-permute-start(bf16[272,512]{1,0:T(8,128)(2,1)S(1)} %shard_map.83.own_kv), channel_id=1, source_target_pairs={{0,8},{4,12},{8,16},{12,20},{16,24},{20,28},{1,9},{5,13},{9,17},{1... | collective-permute-start | bytes 835592 | tf_op jit(solution)/shard_map/ppermute | solution.py:598
  5.1 16.1 %collective-permute-start.3 = (bf16[272,512]{1,0:T(8,128)(2,1)S(1)}, bf16[272,512]{1,0:T(8,128)(2,1)S(1)}, u32[]{:S(2)}, u32[]{:S(2)}) collective-permute-start(bf16[272,512]{1,0:T(8,128)(2,1)S(1)} %get-tuple-element.51), channel_id=1, source_target_pairs={{0,12},{4,8},{8,20},{12,16},{16,28},{20,24},{1,13},{5,9},{9,21},{1... | collective-permute-start | bytes 835592 | tf_op jit(solution)/shard_map/ppermute | solution.py:599
  15.3 14.2 %collective-permute-start.4 = (bf16[256,512]{1,0:T(8,128)(2,1)S(1)}, bf16[256,512]{1,0:T(8,128)(2,1)S(1)}, u32[]{:S(2)}, u32[]{:S(2)}) collective-permute-start(bf16[256,512]{1,0:T(8,128)(2,1)S(1)} %slice.6), channel_id=1, source_target_pairs={{0,8},{4,12},{8,16},{12,20},{16,24},{20,28},{1,9},{5,13},{9,17},{1... | collective-permute-start | bytes 786440 | tf_op jit(solution)/shard_map/ppermute | solution.py:627
  21.2 15.4 %collective-permute-start.5 = (bf16[256,512]{1,0:T(8,128)(2,1)S(1)}, bf16[256,512]{1,0:T(8,128)(2,1)S(1)}, u32[]{:S(2)}, u32[]{:S(2)}) collective-permute-start(bf16[256,512]{1,0:T(8,128)(2,1)S(1)} %slice.8), channel_id=1, source_target_pairs={{0,8},{4,12},{8,16},{12,20},{16,24},{20,28},{1,9},{5,13},{9,17},{1... | collective-permute-start | bytes 786440 | tf_op jit(solution)/shard_map/ppermute | solution.py:628
  22.6 17.6 %collective-permute-start.1 = (bf16[256,512]{1,0:T(8,128)(2,1)S(1)}, bf16[256,512]{1,0:T(8,128)(2,1)S(1)}, u32[]{:S(2)}, u32[]{:S(2)}) collective-permute-start(bf16[256,512]{1,0:T(8,128)(2,1)S(1)} %shard_map.85), channel_id=1, source_target_pairs={{0,24},{4,28},{1,25},{5,29},{2,26},{6,30},{3,27},{7,31}} | collective-permute-start | bytes 786440 | tf_op jit(solution)/shard_map/ppermute | solution.py:664
  42.5 5.0 %collective-permute-start.6 = (bf16[128,512]{1,0:T(8,128)(2,1)S(1)}, bf16[128,512]{1,0:T(8,128)(2,1)S(1)}, u32[]{:S(2)}, u32[]{:S(2)}) collective-permute-start(bf16[128,512]{1,0:T(8,128)(2,1)S(1)} %get-tuple-element.72), channel_id=1, source_target_pairs={{0,4},{4,0},{8,12},{12,8},{16,20},{20,16},{24,28},{28,24},{1,5},{5... | collective-permute-start | bytes 393224 | tf_op jit(solution)/shard_map/ppermute | solution.py:717
  48.0 2.7 %collective-permute-start.8 = (bf16[128,1024]{1,0:T(8,128)(2,1)S(1)}, bf16[128,1024]{1,0:T(8,128)(2,1)S(1)}, u32[]{:S(2)}, u32[]{:S(2)}) collective-permute-start(bf16[128,1024]{1,0:T(8,128)(2,1)S(1)} %get-tuple-element.80), channel_id=1, source_target_pairs={{0,1},{1,0},{2,3},{3,2},{4,5},{5,4},{6,7},{7,6},{8,9},{9,8},{10,11... | collective-permute-start | bytes 786440 | tf_op jit(solution)/shard_map/ppermute | solution.py:744
  50.1 2.2 %collective-permute-start.7 = (bf16[128,1024]{1,0:T(8,128)(2,1)S(1)}, bf16[128,1024]{1,0:T(8,128)(2,1)S(1)}, u32[]{:S(2)}, u32[]{:S(2)}) collective-permute-start(bf16[128,1024]{1,0:T(8,128)(2,1)S(1)} %get-tuple-element.77), channel_id=1, source_target_pairs={{0,1},{1,0},{2,3},{3,2},{4,5},{5,4},{6,7},{7,6},{8,9},{9,8},{10,11... | collective-permute-start | bytes 786440 | tf_op jit(solution)/shard_map/ppermute | solution.py:756
  50.7 8.3 %collective-permute-start.9 = (bf16[128,1024]{1,0:T(8,128)(2,1)S(1)}, bf16[128,1024]{1,0:T(8,128)(2,1)S(1)}, u32[]{:S(2)}, u32[]{:S(2)}) collective-permute-start(bf16[128,1024]{1,0:T(8,128)(2,1)S(1)} %add_convert_fusion.1), channel_id=1, source_target_pairs={{0,2},{1,3},{2,0},{3,1},{4,6},{5,7},{6,4},{7,5},{8,10},{9,11},{10,... | collective-permute-start | bytes 786440 | tf_op jit(solution)/shard_map/ppermute | solution.py:746

commit v2 on v1

--- a/solution.py
+++ b/solution.py
@@ -14,6 +14,7 @@
 KCONV = 11
 MAXBACK = 5
 HALO = 16
+TAIL = 8
 NEG = -1e30
 FLOOR = -5e29
 INSET = 16
@@ -42,9 +43,9 @@
     own = pl.ds(pl.multiple_of(side * half, half), half)
     copy_all(
         [
-            (k_ref.at[:, own], own_kv.at[HALO : HALO + rows, :]),
-            (v_ref.at[:, own], own_kv.at[HALO + rows : HALO + 2 * rows, :]),
-            (q_ref.at[rows - HALO : rows, own], own_kv.at[0:HALO, :]),
+            (k_ref.at[:, own], own_kv.at[TAIL : TAIL + rows, :]),
+            (v_ref.at[:, own], own_kv.at[TAIL + rows : TAIL + 2 * rows, :]),
+            (q_ref.at[rows - TAIL : rows, own], own_kv.at[0:TAIL, :]),
         ],
         sems,
     )
@@ -58,9 +59,9 @@
     oth = pl.ds(pl.multiple_of((1 - side) * half, half), half)
     copy_all(
         [
-            (k_ref.at[:, oth], oth_kv.at[HALO : HALO + rows, :]),
-            (v_ref.at[:, oth], oth_kv.at[HALO + rows : HALO + 2 * rows, :]),
-            (q_ref.at[rows - HALO : rows, oth], oth_kv.at[0:HALO, :]),
+            (k_ref.at[:, oth], oth_kv.at[TAIL : TAIL + rows, :]),
+            (v_ref.at[:, oth], oth_kv.at[TAIL + rows : TAIL + 2 * rows, :]),
+            (q_ref.at[rows - TAIL : rows, oth], oth_kv.at[0:TAIL, :]),
             (q_ref.at[:, oth], oth_all.at[0:rows, :]),
             (k_ref.at[:, oth], oth_all.at[rows : 2 * rows, :]),
             (v_ref.at[:, oth], oth_all.at[2 * rows : 3 * rows, :]),
@@ -260,7 +261,7 @@
 
     @pl.when(side == 1)
     def _():
-        out_ref[...] = own_kv[HALO : HALO + 2 * rows, :]
+        out_ref[...] = own_kv[TAIL : TAIL + 2 * rows, :]
 
 
 def own_kernel(
@@ -278,7 +279,7 @@
     for blk in (0, 1, 8):
         ks[blk * rows : (blk + 1) * rows, :] = zero
         vs[blk * rows : (blk + 1) * rows, :] = zero
-    put(own_kv, HALO, ks, vs, 6 + side)
+    put(own_kv, TAIL, ks, vs, 6 + side)
     put(swap, rows, ks, vs, 7 - side)
     peak[...] = jnp.full(peak.shape, FLOOR, jnp.float32)
     total[...] = jnp.zeros(total.shape, jnp.float32)
@@ -298,16 +299,16 @@
     rows = (qs.shape[0] - HALO) // 2
     side, first = place()
     first_row = first * rows
-    put(pa, HALO, ks, vs, 4 + side)
-    put(pb, HALO, ks, vs, 5 - side)
+    put(pa, TAIL, ks, vs, 4 + side)
+    put(pb, TAIL, ks, vs, 5 - side)
 
     @pl.when(side == 0)
     def _():
-        qs[0:HALO, :] = pb[0:HALO, :]
+        qs[HALO - TAIL : HALO, :] = pb[0:TAIL, :]
 
     @pl.when(side == 1)
     def _():
-        qs[0:HALO, :] = pa[0:HALO, :]
+        qs[HALO - TAIL : HALO, :] = pa[0:TAIL, :]
 
     state = (peak, total, acc)
     window_masks(first_row - 2 * rows, first_row, 0, 2 * rows, start, score_ok, bias)
@@ -413,6 +414,11 @@
         out_ref[n] = jnp.dot(x_ref[...], w_ref[n], preferred_element_type=jnp.float32)
     for copy in copies:
         copy.wait()
+
+
+def one_part_kernel(x_ref, w_ref, part_ref, out_ref, *, n):
+    out = jnp.dot(x_ref[...], w_ref[n], preferred_element_type=jnp.float32)
+    out_ref[...] = (out + part_ref[n]).astype(jnp.bfloat16)
 
 
 def late_part_kernel(x_ref, out_weight, part_ref, give_ref, keep_ref, w_near, sems):
@@ -561,7 +567,7 @@
     small = pltpu.CompilerParams(vmem_limit_bytes=8 * 1024 * 1024)
     bf = jnp.bfloat16
     f32 = jnp.float32
-    kv_rows = 2 * rows + HALO
+    kv_rows = 2 * rows + TAIL
     n_rows = 2 * rows
     n_ext = n_rows + HALO
     on_chip = pltpu.VMEM
@@ -591,6 +597,7 @@
 
     pairs = range(n_pb)
     up = [(i, i + 2) for i in pairs if i + 2 < n_pb]
+    onward = [(i, j) for i, j in up if i >= 2]
     cross = [(i, (i ^ 1) + 2) for i in pairs if (i ^ 1) + 2 < n_pb]
     swap_route = [(i, i ^ 1) for i in pairs]
     far = [(i, i + MAXBACK + 1) for i in pairs if i + MAXBACK + 1 < n_pb]
@@ -624,8 +631,8 @@
         ),
     )(stay(turn_lengths), stay(theta.transpose(1, 0, 2)), stay(mix.T), stay(gain.reshape(1, -1)), heavy)
     pa, w = lax.optimization_barrier((pa, w))
-    fa = lax.ppermute(pa[HALO:], "pb", up)
-    fb = lax.ppermute(pbk[HALO:], "pb", up)
+    fa = lax.ppermute(pa[TAIL:], "pb", onward)
+    fb = lax.ppermute(pbk[TAIL:], "pb", onward)
 
     def state(make):
         return (
@@ -733,14 +740,19 @@
     )
 
     near_route = [(i, i ^ 1) for i in range(n_ha)]
-    give, keep = pl.pallas_call(
-        functools.partial(add_part_kernel, lo=0),
-        out_shape=halves,
-        in_specs=[vm, vm, vm],
-        out_specs=(vm, vm),
-        compiler_params=params,
-        cost_estimate=half_cost,
-    )(got, w_far, own_part)
+
+    def far_part(n):
+        return pl.pallas_call(
+            functools.partial(one_part_kernel, n=n),
+            out_shape=halves[n],
+            in_specs=[vm, vm, vm],
+            out_specs=vm,
+            compiler_params=params,
+            cost_estimate=half_cost,
+        )(got, w_far, own_part)
+
+    give = far_part(0)
+    keep = far_part(1)
     take = lax.ppermute(give, "ha", near_route)
     away = (keep.astype(f32) + take.astype(f32)).astype(bf)
     arrived = lax.ppermute(away, "ha", [(i, i ^ 2) for i in range(n_ha)])

time: 60.2 us -> 59.9 us (level)
  the two profiles are of different devices: /device:TPU:24 before, /device:TPU:28 now
where the time goes in v2:
time: 59.9 us; the launch traced here: 59.5 us
  waiting for transfers between devices  27.2 us (45%)
  Pallas kernels  21.4 us (36%)
  starting transfers between devices  9.77 us (16%)
  other arithmetic  0.89 us (1%)
    ppermute x1, waiting for transfers between devices, paired_plan(): arrived = lax.ppermute(away, 'ha', [(i, i ^ 2) for i in range(n_ha)])  7.55 us
    ppermute x1, waiting for transfers between devices, paired_plan(): fb = lax.ppermute(pbk[TAIL:], 'pb', onward)  7.02 us
    ppermute x1, waiting for transfers between devices, paired_plan(): pa = lax.ppermute(own_kv, 'pb', up)  5.29 us
    ppermute x1, waiting for transfers between devices, paired_plan(): pbk = lax.ppermute(oth_kv, 'pb', cross)  4.44 us
    pallas_call x1, Pallas kernels, paired_plan(): pl.pallas_call(functools.partial(prep_kernel, scale=1.0 / math.sqrt(dh)),...  3.35 us
    pallas_call x1, Pallas kernels, paired_plan(): pl.pallas_call(mid_kernel, out_shape=(span, span) + state(on_chip), in_sp...  2.83 us
    pallas_call x1, Pallas kernels, paired_plan(): pl.pallas_call(next_kernel, out_shape=(on_chip((n_ext, half), bf), span,...  2.68 us
    pallas_call x1, Pallas kernels, paired_plan(): pl.pallas_call(own_kernel, out_shape=(on_chip((n_ext, half), bf), span, s...  2.66 us
  transfers between devices with their start and end apart: 10, of which 7 were waited for; matrix products, arithmetic and copies ran while one was open for 0% of the time, Pallas kernels for 30%

profile of v2, /device:TPU:28, one launch (start us, length us, event | category | flops | bytes accessed | tf_op | source)
XLA Modules:
  0.0 59.5 jit_solution(14555200619595427677)
XLA Ops:
  0.0 1.3 %shard_map.84 = (bf16[128,512]{1,0:T(8,128)(2,1)S(1)}, bf16[384,512]{1,0:T(8,128)(2,1)S(1)}, bf16[264,512]{1,0:T(8,128)(2,1)S(1)}) custom-call(bf16[128,1024]{1,0:T(8,128)(2,1)} %q_ref.3, bf16[128,1024]{1,0:T(8,128)(2,1)} %k_ref.3, bf16[128,1024]{1,0:T(8,128)(2,1)} %v_ref.3), custom_call_target="tpu_custom_call" | custom-call | tf_op jit(solution)/shard_map/pallas_call | solution.py:585
  1.3 1.6 %collective-permute-start = (bf16[384,512]{1,0:T(8,128)(2,1)S(1)}, bf16[384,512]{1,0:T(8,128)(2,1)S(1)}, u32[]{:S(2)}, u32[]{:S(2)}) collective-permute-start(bf16[384,512]{1,0:T(8,128)(2,1)S(1)} %get-tuple-element.43), channel_id=1, source_target_pairs={{0,4},{4,0},{8,12},{12,8},{16,20},{20,16},{24,28},{28,24},{1,5},{5... | collective-permute-start | bytes 1179656 | tf_op jit(solution)/shard_map/ppermute | solution.py:607
  2.8 1.0 %shard_map.83.own_kv = bf16[264,512]{1,0:T(8,128)(2,1)S(1)} custom-call(bf16[128,1024]{1,0:T(8,128)(2,1)} %q_ref.3, bf16[128,1024]{1,0:T(8,128)(2,1)} %k_ref.3, bf16[128,1024]{1,0:T(8,128)(2,1)} %v_ref.3), custom_call_target="tpu_custom_call" | custom-call | tf_op jit(solution)/shard_map/pallas_call | solution.py:577
  3.8 1.3 %collective-permute-start.2 = (bf16[264,512]{1,0:T(8,128)(2,1)S(1)}, bf16[264,512]{1,0:T(8,128)(2,1)S(1)}, u32[]{:S(2)}, u32[]{:S(2)}) collective-permute-start(bf16[264,512]{1,0:T(8,128)(2,1)S(1)} %shard_map.83.own_kv), channel_id=1, source_target_pairs={{0,8},{4,12},{8,16},{12,20},{16,24},{20,28},{1,9},{5,13},{9,17},{1... | collective-permute-start | bytes 811016 | tf_op jit(solution)/shard_map/ppermute | solution.py:605
  5.1 1.3 %collective-permute-start.3 = (bf16[264,512]{1,0:T(8,128)(2,1)S(1)}, bf16[264,512]{1,0:T(8,128)(2,1)S(1)}, u32[]{:S(2)}, u32[]{:S(2)}) collective-permute-start(bf16[264,512]{1,0:T(8,128)(2,1)S(1)} %get-tuple-element.49), channel_id=1, source_target_pairs={{0,12},{4,8},{8,20},{12,16},{16,28},{20,24},{1,13},{5,9},{9,21},{1... | collective-permute-start | bytes 811016 | tf_op jit(solution)/shard_map/ppermute | solution.py:606
  6.4 3.3 %shard_map.82 = (bf16[12,256,256]{2,1,0:T(8,128)(2,1)S(1)}, s32[272,128]{1,0:T(8,128)S(1)}, f32[5,256,128]{2,1,0:T(8,128)S(1)}, bf16[4,512,1024]{2,1,0:T(8,128)(...) custom-call(s32[16]{0:T(128)} %len_ref.1, f32[6,8,11]{2,1,0:T(8,128)} %bitcast.3, f32[4,8]{1,0:T(4,128)} %bitcast.5, ...), custom_call_target="tpu_custom_call" | custom-call | flops 20000000 | bytes 2400000 | tf_op jit(solution)/shard_map/pallas_call | solution.py:615
  9.8 5.3 %collective-permute-done.2.pa = bf16[264,512]{1,0:T(8,128)(2,1)S(1)} collective-permute-done((bf16[264,512]{1,0:T(8,128)(2,1)S(1)}, bf16[264,512]{1,0:T(8,128)(2,1)S(1)}, u32[]{:S(2)}, u32[]{:S(2)}) %collective-permute-start.2) | collective-permute-done | bytes 270368 | tf_op jit(solution)/shard_map/ppermute | solution.py:605
  15.1 1.3 %collective-permute-start.4 = (bf16[256,512]{1,0:T(8,128)(2,1)S(1)}, bf16[256,512]{1,0:T(8,128)(2,1)S(1)}, u32[]{:S(2)}, u32[]{:S(2)}) collective-permute-start(bf16[256,512]{1,0:T(8,128)(2,1)S(1)} %slice.6), channel_id=1, source_target_pairs={{8,16},{12,20},{16,24},{20,28},{9,17},{13,21},{17,25},{21,29},{10,... | collective-permute-start | bytes 786440 | tf_op jit(solution)/shard_map/ppermute | solution.py:634
  16.4 4.4 %collective-permute-done.3.pb = bf16[264,512]{1,0:T(8,128)(2,1)S(1)} collective-permute-done((bf16[264,512]{1,0:T(8,128)(2,1)S(1)}, bf16[264,512]{1,0:T(8,128)(2,1)S(1)}, u32[]{:S(2)}, u32[]{:S(2)}) %collective-permute-start.3) | collective-permute-done | bytes 270368 | tf_op jit(solution)/shard_map/ppermute | solution.py:606
  20.9 1.3 %collective-permute-start.5 = (bf16[256,512]{1,0:T(8,128)(2,1)S(1)}, bf16[256,512]{1,0:T(8,128)(2,1)S(1)}, u32[]{:S(2)}, u32[]{:S(2)}) collective-permute-start(bf16[256,512]{1,0:T(8,128)(2,1)S(1)} %slice.8), channel_id=1, source_target_pairs={{8,16},{12,20},{16,24},{20,28},{9,17},{13,21},{17,25},{21,29},{10,... | collective-permute-start | bytes 786440 | tf_op jit(solution)/shard_map/ppermute | solution.py:635
  22.2 0.0 collective-permute-done.swap
  22.2 1.3 %collective-permute-start.1 = (bf16[256,512]{1,0:T(8,128)(2,1)S(1)}, bf16[256,512]{1,0:T(8,128)(2,1)S(1)}, u32[]{:S(2)}, u32[]{:S(2)}) collective-permute-start(bf16[256,512]{1,0:T(8,128)(2,1)S(1)} %shard_map.85), channel_id=1, source_target_pairs={{0,24},{4,28},{1,25},{5,29},{2,26},{6,30},{3,27},{7,31}} | collective-permute-start | bytes 786440 | tf_op jit(solution)/shard_map/ppermute | solution.py:671
  23.5 2.7 %shard_map.86 = (bf16[272,512]{1,0:T(8,128)(2,1)S(1)}, bf16[1152,512]{1,0:T(8,128)(2,1)S(1)}, bf16[1152,512]{1,0:T(8,128)(2,1)S(1)}, f32[4,256,128]{2,1,0:T(8,12...) custom-call(bf16[128,512]{1,0:T(8,128)(2,1)S(1)} %get-tuple-element.50.own_q, ...), custom_call_target="tpu_custom_call" | custom-call | flops 1500000000 | bytes 6000000 | tf_op jit(solution)/shard_map/pallas_call | solution.py:672
  26.2 2.7 %shard_map.87 = (bf16[272,512]{1,0:T(8,128)(2,1)S(1)}, bf16[1152,512]{1,0:T(8,128)(2,1)S(1)}, bf16[1152,512]{1,0:T(8,128)(2,1)S(1)}, f32[4,256,128]{2,1,0:T(8,12...) custom-call(bf16[264,512]{1,0:T(8,128)(2,1)S(1)} %collective-permute, ...), custom_call_target="tpu_custom_call", output_to_operand_aliasing={{0}: (5, {}), {1}: (6, {}), {2}: (7, {}), {3}: (8, {}), {4}... | custom-call | flops 1500000000 | bytes 6000000 | tf_op jit(solution)/shard_map/pallas_call | solution.py:683
  28.9 0.4 collective-permute-done.4.fa
  29.3 7.0 %collective-permute-done.5.fb = bf16[256,512]{1,0:T(8,128)(2,1)S(1)} collective-permute-done((bf16[256,512]{1,0:T(8,128)(2,1)S(1)}, bf16[256,512]{1,0:T(8,128)(2,1)S(1)}, u32[]{:S(2)}, u32[]{:S(2)}) %collective-permute-start.5) | collective-permute-done | bytes 262176 | tf_op jit(solution)/shard_map/ppermute | solution.py:635
  36.3 2.8 %shard_map.88 = (bf16[1152,512]{1,0:T(8,128)(2,1)S(1)}, bf16[1152,512]{1,0:T(8,128)(2,1)S(1)}, f32[4,256,128]{2,1,0:T(8,128)S(1)}, f32[4,256,128]{2,1,0:T(8,128)S(1)}, f32[4,256,512]{2,1,0:T(8,128)S(1)}) custom-call(bf16[256,512]{1,0:T(8,128)(2,1)S(1)} %collective-permute-done.4.fa, ...), custom_call_target="tpu_custom_call", output_to_operand_aliasing={{0}: (6, {}), {1}: (7, {}), {2}: (8, {}), {3}: (9, {}), {4}... | custom-call | flops 1500000000 | bytes 6000000 | tf_op jit(solution)/shard_map/pallas_call | solution.py:693
  39.2 0.5 shard_map.89.odd_ref
  39.7 0.0 collective-permute-done.1.last
  39.7 2.2 %shard_map.90 = (bf16[128,512]{1,0:T(8,128)(2,1)S(1)}, bf16[128,512]{1,0:T(8,128)(2,1)S(1)}, bf16[1152,512]{1,0:T(8,128)(2,1)S(1)}, bf16[1152,512]{1,0:T(8,128)(2,1)S(1)}) custom-call(f32[16,128]{1,0:T(8,128)S(1)} %get-tuple-element.41.mix_ref, f32[1,512]{1,0:T(1,128)S(1)} %get-tuple-element.42.gain_ref, ...), custom_call_target="tpu_custom_call", output_to_operand_aliasing={{2}: (8, {}), {3}: (9, {})} | custom-call | flops 750000000 | bytes 3000000 | tf_op jit(solution)/shard_map/pallas_call | solution.py:714
  41.9 0.6 collective-permute-start.6
  42.5 2.2 %shard_map.91 = (f32[4,128,1024]{2,1,0:T(8,128)S(1)}, bf16[2,512,1024]{2,1,0:T(8,128)(2,1)S(1)}) custom-call(bf16[128,512]{1,0:T(8,128)(2,1)S(1)} %get-tuple-element.71.x_ref, bf16[4,512,1024]{2,1,0:T(8,128)(2,1)S(1)} %get-tuple-element.72.w_ref, bf16[1024,4096]{1,0:T(8,128)(2,1)} %out_weight.5), custom_call_target="tpu_custom_call" | custom-call | flops 536870912 | bytes 8000000 | tf_op jit(solution)/shard_map/pallas_call | solution.py:726
  44.7 2.3 %collective-permute-done.6.x_ref = bf16[128,512]{1,0:T(8,128)(2,1)S(1)} collective-permute-done((bf16[128,512]{1,0:T(8,128)(2,1)S(1)}, bf16[128,512]{1,0:T(8,128)(2,1)S(1)}, u32[]{:S(2)}, u32[]{:S(2)}) %collective-permute-start.6) | collective-permute-done | bytes 131104 | tf_op jit(solution)/shard_map/ppermute | solution.py:724
  47.0 0.3 shard_map.94
  47.3 0.1 collective-permute-start.8
  47.4 2.0 %shard_map.92 = (bf16[128,1024]{1,0:T(8,128)(2,1)S(1)}, bf16[128,1024]{1,0:T(8,128)(2,1)S(1)}) custom-call(bf16[128,512]{1,0:T(8,128)(2,1)S(1)} %collective-permute-done.6.x_ref, bf16[1024,4096]{1,0:T(8,128)(2,1)} %out_weight.5, f32[4,128,1024]{2,1,0:T(8,128)S(1)} %get-tuple-element.73.part_ref), custom_call_target="tpu_custom_call" | custom-call | flops 268435456 | bytes 4000000 | tf_op jit(solution)/shard_map/pallas_call | solution.py:759
  49.4 0.5 collective-permute-start.7
  50.0 0.3 shard_map.93
  50.3 0.0 collective-permute-done.8
  50.3 0.1 add_convert_fusion.1
  50.4 0.6 collective-permute-start.9
  50.9 0.2 collective-permute-done.7
  51.1 7.5 %collective-permute-done.9 = bf16[128,1024]{1,0:T(8,128)(2,1)S(1)} collective-permute-done((bf16[128,1024]{1,0:T(8,128)(2,1)S(1)}, bf16[128,1024]{1,0:T(8,128)(2,1)S(1)}, u32[]{:S(2)}, u32[]{:S(2)}) %collective-permute-start.9) | collective-permute-done | bytes 262176 | tf_op jit(solution)/shard_map/ppermute | solution.py:758
  58.7 0.8 %add_convert_fusion = bf16[128,1024]{1,0:T(8,128)(2,1)} fusion(bf16[128,1024]{1,0:T(8,128)(2,1)S(1)} %collective-permute-done.9, bf16[128,1024]{1,0:T(8,128)(2,1)S(1)} %collective-permute-done.7, bf16[128,1024]{1,0:T(8,128)(2,1)S(1)} %get-tuple-element.74), kind=kLoop, calls=%fused_computation | loop fusion | flops 786432 | bytes 1048576 | tf_op jit(solution)/shard_map/convert_element_type | solution.py:770
  (3 shorter events, 0.1 us)
Async XLA Ops:
  1.3 20.9 %collective-permute-start = (bf16[384,512]{1,0:T(8,128)(2,1)S(1)}, bf16[384,512]{1,0:T(8,128)(2,1)S(1)}, u32[]{:S(2)}, u32[]{:S(2)}) collective-permute-start(bf16[384,512]{1,0:T(8,128)(2,1)S(1)} %get-tuple-element.43), channel_id=1, source_target_pairs={{0,4},{4,0},{8,12},{12,8},{16,20},{20,16},{24,28},{28,24},{1,5},{5... | collective-permute-start | bytes 1179656 | tf_op jit(solution)/shard_map/ppermute | solution.py:607
  3.8 11.2 %collective-permute-start.2 = (bf16[264,512]{1,0:T(8,128)(2,1)S(1)}, bf16[264,512]{1,0:T(8,128)(2,1)S(1)}, u32[]{:S(2)}, u32[]{:S(2)}) collective-permute-start(bf16[264,512]{1,0:T(8,128)(2,1)S(1)} %shard_map.83.own_kv), channel_id=1, source_target_pairs={{0,8},{4,12},{8,16},{12,20},{16,24},{20,28},{1,9},{5,13},{9,17},{1... | collective-permute-start | bytes 811016 | tf_op jit(solution)/shard_map/ppermute | solution.py:605
  5.1 15.7 %collective-permute-start.3 = (bf16[264,512]{1,0:T(8,128)(2,1)S(1)}, bf16[264,512]{1,0:T(8,128)(2,1)S(1)}, u32[]{:S(2)}, u32[]{:S(2)}) collective-permute-start(bf16[264,512]{1,0:T(8,128)(2,1)S(1)} %get-tuple-element.49), channel_id=1, source_target_pairs={{0,12},{4,8},{8,20},{12,16},{16,28},{20,24},{1,13},{5,9},{9,21},{1... | collective-permute-start | bytes 811016 | tf_op jit(solution)/shard_map/ppermute | solution.py:606
  15.1 14.2 %collective-permute-start.4 = (bf16[256,512]{1,0:T(8,128)(2,1)S(1)}, bf16[256,512]{1,0:T(8,128)(2,1)S(1)}, u32[]{:S(2)}, u32[]{:S(2)}) collective-permute-start(bf16[256,512]{1,0:T(8,128)(2,1)S(1)} %slice.6), channel_id=1, source_target_pairs={{8,16},{12,20},{16,24},{20,28},{9,17},{13,21},{17,25},{21,29},{10,... | collective-permute-start | bytes 786440 | tf_op jit(solution)/shard_map/ppermute | solution.py:634
  20.9 15.4 %collective-permute-start.5 = (bf16[256,512]{1,0:T(8,128)(2,1)S(1)}, bf16[256,512]{1,0:T(8,128)(2,1)S(1)}, u32[]{:S(2)}, u32[]{:S(2)}) collective-permute-start(bf16[256,512]{1,0:T(8,128)(2,1)S(1)} %slice.8), channel_id=1, source_target_pairs={{8,16},{12,20},{16,24},{20,28},{9,17},{13,21},{17,25},{21,29},{10,... | collective-permute-start | bytes 786440 | tf_op jit(solution)/shard_map/ppermute | solution.py:635
  22.2 17.5 %collective-permute-start.1 = (bf16[256,512]{1,0:T(8,128)(2,1)S(1)}, bf16[256,512]{1,0:T(8,128)(2,1)S(1)}, u32[]{:S(2)}, u32[]{:S(2)}) collective-permute-start(bf16[256,512]{1,0:T(8,128)(2,1)S(1)} %shard_map.85), channel_id=1, source_target_pairs={{0,24},{4,28},{1,25},{5,29},{2,26},{6,30},{3,27},{7,31}} | collective-permute-start | bytes 786440 | tf_op jit(solution)/shard_map/ppermute | solution.py:671
  41.9 5.0 %collective-permute-start.6 = (bf16[128,512]{1,0:T(8,128)(2,1)S(1)}, bf16[128,512]{1,0:T(8,128)(2,1)S(1)}, u32[]{:S(2)}, u32[]{:S(2)}) collective-permute-start(bf16[128,512]{1,0:T(8,128)(2,1)S(1)} %get-tuple-element.70), channel_id=1, source_target_pairs={{0,4},{4,0},{8,12},{12,8},{16,20},{20,16},{24,28},{28,24},{1,5},{5... | collective-permute-start | bytes 393224 | tf_op jit(solution)/shard_map/ppermute | solution.py:724
  47.3 3.0 %collective-permute-start.8 = (bf16[128,1024]{1,0:T(8,128)(2,1)S(1)}, bf16[128,1024]{1,0:T(8,128)(2,1)S(1)}, u32[]{:S(2)}, u32[]{:S(2)}) collective-permute-start(bf16[128,1024]{1,0:T(8,128)(2,1)S(1)} %shard_map.94), channel_id=1, source_target_pairs={{0,1},{1,0},{2,3},{3,2},{4,5},{5,4},{6,7},{7,6},{8,9},{9,8},{10,11... | collective-permute-start | bytes 786440 | tf_op jit(solution)/shard_map/ppermute | solution.py:756
  49.4 1.7 %collective-permute-start.7 = (bf16[128,1024]{1,0:T(8,128)(2,1)S(1)}, bf16[128,1024]{1,0:T(8,128)(2,1)S(1)}, u32[]{:S(2)}, u32[]{:S(2)}) collective-permute-start(bf16[128,1024]{1,0:T(8,128)(2,1)S(1)} %get-tuple-element.75), channel_id=1, source_target_pairs={{0,1},{1,0},{2,3},{3,2},{4,5},{5,4},{6,7},{7,6},{8,9},{9,8},{10,11... | collective-permute-start | bytes 786440 | tf_op jit(solution)/shard_map/ppermute | solution.py:768
  50.4 8.3 %collective-permute-start.9 = (bf16[128,1024]{1,0:T(8,128)(2,1)S(1)}, bf16[128,1024]{1,0:T(8,128)(2,1)S(1)}, u32[]{:S(2)}, u32[]{:S(2)}) collective-permute-start(bf16[128,1024]{1,0:T(8,128)(2,1)S(1)} %add_convert_fusion.1), channel_id=1, source_target_pairs={{0,2},{1,3},{2,0},{3,1},{4,6},{5,7},{6,4},{7,5},{8,10},{9,11},{10,... | collective-permute-start | bytes 786440 | tf_op jit(solution)/shard_map/ppermute | solution.py:758
